TPU v7x, 256 devices: a whole 4x4x8 slice. The times are simulated.
256 devices in a mesh: cls: 8 (over x, core), dom: 32 (over z, y).
Axes of the slice: x: 4, y: 4, z: 8, core: 2. Of those that a mesh axis runs over, the one named last changes fastest.
Arguments:
- particles: bfloat16 [1024, 36864], P(('cls', 'dom')), may hold values from -6 to 6
- references: bfloat16 [200, 36864], P('cls'), may hold values from -0.03125 to 0.03125
- candidates: int32 [1024, 8], P(('cls', 'dom')), may hold values from 0 to 199, as said below
- offsets: int32 [1024, 2], P(('cls', 'dom')), may hold values from -7 to 7
Outputs:
- class_average: bfloat16 [200, 36864], P('cls')
Inputs may be any that keep to these rules, and one draw needn't show every extreme that they name: `candidates`: each particle lists 8 distinct classes, 4 of them with each of two class owners, the owner of class c being c // (200 / number of cls groups). Of the 4 particles of one device at most 2 list classes of one owner, and on every device some owner is listed by exactly 2.
All inputs are finite; a program needn't handle non-finite values.
Results may differ from a plain program's by a relative error of at most 0.0074.
Values may be sent and summed in bfloat16 or wider, within the bound.
A program may use at most 128 MiB of HBM per device.

v0:
```python
import math

import jax
import jax.numpy as jnp
from jax import lax
from jax.sharding import PartitionSpec as P

CYCLES = 128
ANGLES = 144
ROT = 36
SHIFTS = 5
BOX = 256


SOFTMAX_WARMTH = 2.0
PRIOR_MASS = 1.0
NEGATIVE = -1e30
SHIFT_X_STEPS = (0, 1, -1, 0, 0)
SHIFT_Y_STEPS = (0, 0, 0, 1, -1)


def phase_angles(move_x, move_y):
    theta = 2.0 * math.pi * jnp.arange(ANGLES, dtype=jnp.float32) / ANGLES
    radius = jnp.arange(1, CYCLES + 1, dtype=jnp.float32)
    along = (
        jnp.cos(theta)[:, None] * move_x.astype(jnp.float32)[..., None, None]
        + jnp.sin(theta)[:, None] * move_y.astype(jnp.float32)[..., None, None]
    )
    return 2.0 * math.pi / BOX * along * radius


def shift_images(images, phase):
    real_part = images[..., 0, :].astype(jnp.float32)
    imag_part = images[..., 1, :].astype(jnp.float32)
    cosine = jnp.cos(phase)
    sine = jnp.sin(phase)
    return jnp.stack(
        [real_part * cosine + imag_part * sine, imag_part * cosine - real_part * sine], axis=-2
    ).astype(jnp.bfloat16)


def shards(particles, references, candidates, offsets):
    groups = lax.axis_size("cls")
    owner = lax.axis_index("cls")
    count = particles.shape[0]
    capacity = count // 2
    local = references.shape[0]
    width = references.shape[1]
    listed_count = candidates.shape[1]
    block_width = width // ROT
    row_count = groups * capacity
    listed_owner = candidates // local
    group_index = jnp.arange(groups, dtype=jnp.int32)
    present = jnp.any(listed_owner[:, :, None] == group_index[None, None, :], axis=1)
    ranking = jnp.cumsum(present.astype(jnp.int32), axis=0) - 1
    slot_index = jnp.arange(capacity, dtype=jnp.int32)
    class_assignment = present.T[:, None, :] & (ranking.T[:, None, :] == slot_index[None, :, None])
    outgoing = jnp.einsum(
        "evd,do->evo",
        class_assignment.astype(jnp.bfloat16),
        particles,
        preferred_element_type=jnp.float32,
    ).astype(jnp.bfloat16)
    particle_index = jnp.arange(count, dtype=jnp.int32)
    particle_records = jnp.concatenate(
        [
            candidates.astype(jnp.float32),
            offsets.astype(jnp.float32),
            particle_index[:, None].astype(jnp.float32),
            jnp.ones((count, 1), jnp.float32),
            jnp.zeros((count, 4), jnp.float32),
        ],
        axis=1,
    )
    meta_out = jnp.einsum(
        "yhu,um->yhm",
        class_assignment.astype(jnp.float32),
        particle_records,
        precision=lax.Precision.HIGHEST,
    ).astype(jnp.bfloat16)
    arrived, arrived_meta = (
        lax.all_to_all(outgoing, "cls", split_axis=0, concat_axis=0, tiled=True),
        lax.all_to_all(meta_out, "cls", split_axis=0, concat_axis=0, tiled=True),
    )
    details = arrived_meta.astype(jnp.float32).reshape(row_count, -1)
    listed = details[:, :listed_count].astype(jnp.int32)
    prior_x = details[:, listed_count].astype(jnp.int32)
    prior_y = details[:, listed_count + 1].astype(jnp.int32)
    filled = details[:, listed_count + 3] > 0.5
    class_index = owner * local + jnp.arange(local, dtype=jnp.int32)
    allowed = jnp.any(listed[:, :, None] == class_index[None, None, :], axis=1) & filled[:, None]
    turn_index = jnp.arange(ROT, dtype=jnp.int32)
    diagonal = (
        turn_index[None, :, None] == (turn_index[:, None, None] - turn_index[None, None, :]) % ROT
    )
    diagonal_f32 = diagonal.astype(jnp.float32)
    diagonal_bf16 = diagonal.astype(jnp.bfloat16)
    class_refs = references.reshape(local, ROT, block_width)
    images = arrived.reshape(row_count, ANGLES, 2, CYCLES)
    moved_list = []
    score_list = []
    for shift in range(SHIFTS):
        phase = phase_angles(prior_x + SHIFT_X_STEPS[shift], prior_y + SHIFT_Y_STEPS[shift])
        moved = shift_images(images, phase).reshape(row_count, ROT, block_width)
        pairs = jnp.einsum("xjf,clf->xjcl", moved, class_refs, preferred_element_type=jnp.float32)
        score_values = SOFTMAX_WARMTH * jnp.einsum(
            "xjcl,jlr->xcr", pairs, diagonal_f32, precision=lax.Precision.HIGHEST
        )
        moved_list.append(moved)
        score_list.append(score_values)
    all_scores = jnp.stack(score_list, axis=1)
    allowed_wide = allowed[:, None, :, None]
    local_max = jnp.max(jnp.where(allowed_wide, all_scores, NEGATIVE), axis=(1, 2, 3))
    local_sum = jnp.sum(
        jnp.exp(jnp.where(allowed_wide, all_scores - local_max[:, None, None, None], NEGATIVE)),
        axis=(1, 2, 3),
    )
    back_max, back_sum = (
        lax.all_to_all(
            local_max.reshape(groups, capacity), "cls", split_axis=0, concat_axis=0, tiled=True
        ),
        lax.all_to_all(
            local_sum.reshape(groups, capacity), "cls", split_axis=0, concat_axis=0, tiled=True
        ),
    )
    owner_max = jnp.max(jnp.where(class_assignment, back_max[:, :, None], NEGATIVE), axis=1)
    owner_sum = jnp.sum(jnp.where(class_assignment, back_sum[:, :, None], 0.0), axis=1)
    whole_max = jnp.max(owner_max, axis=0)
    whole_sum = jnp.sum(owner_sum * jnp.exp(owner_max - whole_max[None, :]), axis=0)
    slot_max = jnp.sum(jnp.where(class_assignment, whole_max[None, None, :], 0.0), axis=2)
    slot_sum = jnp.sum(jnp.where(class_assignment, whole_sum[None, None, :], 0.0), axis=2)
    total_max, total_sum = (
        lax.all_to_all(slot_max, "cls", split_axis=0, concat_axis=0, tiled=True),
        lax.all_to_all(slot_sum, "cls", split_axis=0, concat_axis=0, tiled=True),
    )
    total_max = total_max.reshape(row_count)
    total_sum = total_sum.reshape(row_count)
    safe_sum = jnp.where(filled, total_sum, 1.0)
    totals = jnp.zeros((local, ROT, block_width), jnp.float32)
    masses = jnp.zeros((local,), jnp.float32)
    for shift in range(SHIFTS):
        exponent = jnp.exp(
            jnp.where(allowed[:, :, None], score_list[shift] - total_max[:, None, None], NEGATIVE)
        )
        weight = (exponent / safe_sum[:, None, None]).astype(jnp.bfloat16)
        masses = masses + jnp.sum(weight.astype(jnp.float32), axis=(0, 2))
        spread = jnp.einsum(
            "xcr,jlr->xcjl", weight, diagonal_bf16, preferred_element_type=jnp.float32
        ).astype(jnp.bfloat16)
        totals = totals + jnp.einsum(
            "xcjl,xjf->clf", spread, moved_list[shift], preferred_element_type=jnp.float32
        )
    totals = totals.reshape(local, width)
    summed, summed_mass = lax.psum((totals, masses), "dom")
    return (summed / (summed_mass + PRIOR_MASS)[:, None]).astype(jnp.bfloat16)


def solution(mesh):
    in_specs = (
        P(("cls", "dom"), None),
        P("cls", None),
        P(("cls", "dom"), None),
        P(("cls", "dom"), None),
    )
    out_specs = P("cls", None)
    return jax.shard_map(shards, mesh=mesh, in_specs=in_specs, out_specs=out_specs, check_vma=False)
```

profile of v0, /device:TPU:8, one launch (start us, length us, event | category | flops | bytes accessed | tf_op | source)
XLA Modules:
  0.0 399.1 jit_solution(13238544202436421924)
XLA Ops:
  9.1 4.3 %all-to-all-start = ((bf16[8,2,16]{2,1,0:T(2,128)(2,1)}), bf16[8,2,16]{2,1,0:T(2,128)(2,1)S(1)}, u32[]{:S(2)}, u32[]{:S(2)}) async-start(bf16[8,2,16]{2,1,0:T(2,128)(2,1)} %copy.74), calls=%async_computation | async-start | bytes 8192 | tf_op jit(solution)/shard_map/all_to_all | solution.py:83
  18.6 3.9 all-to-all-start.1
  22.5 4.1 %reshape.607 = bf16[25,36,1024,1]{2,1,0,3:T(8,128)(2,1)} reshape(bf16[25,36864]{1,0:T(8,128)(2,1)} %param.5) | data formatting | bytes 3686400 | tf_op jit(solution)/shard_map/reshape | solution.py:98
  27.4 12.4 %all-to-all-done.1 = bf16[8,2,36864]{2,1,0:T(2,128)(2,1)S(1)} async-done(((bf16[8,2,36864]{2,1,0:T(2,128)(2,1)}), bf16[8,2,36864]{2,1,0:T(2,128)(2,1)S(1)}, u32[]{:S(2)}, u32[]{:S(2)}) %all-to-all-start.1) | async-done | bytes 1179680 | tf_op jit(solution)/shard_map/all_to_all | solution.py:82
  42.3 4.9 %fusion.38 = (bf16[16,144,1,128]{3,1,2,0:T(8,128)(2,1)S(1)}, bf16[16,144,1,128]{3,1,2,0:T(8,128)(2,1)S(1)}, bf16[16,144,1,128]{3,1,2,0:T(8,128)(2,1)S(1)}) fusion(f32[16,144]{1,0:T(8,128)S(1)} %get-tuple-element.58, f32[128]{0:T(128)S(1)} %iota_add_fusion, bf16[16,144,1,128]{3,2,1,0:T(2,128)(2,1)S(1)} %get-tuple-element.46, ...), kind=kLoop, calls=%fused_computation.84 | loop fusion | flops 2064384 | bytes 2958848 | tf_op jit(solution)/shard_map/add | solution.py:38
  47.3 23.6 %fusion.36 = (bf16[16,144,1,128]{3,1,2,0:T(8,128)(2,1)}, bf16[16,144,1,128]{3,1,2,0:T(8,128)(2,1)}, bf16[16,144,1,128]{3,1,2,0:T(8,128)(2,1)}, bf16[16,144,1,128...) fusion(bf16[16,144,1,128]{3,1,2,0:T(8,128)(2,1)S(1)} %get-tuple, ...), kind=kLoop, calls=%fused_computation.82 | loop fusion | flops 12681216 | bytes 6534656 | tf_op jit(solution)/shard_map/add | solution.py:38
  79.0 3.1 reshape.610
  82.2 9.4 %fusion.30 = f32[16,36,25,36]{3,1,2,0:T(8,128)} fusion(bf16[25,36,1024,1]{2,1,0,3:T(8,128)(2,1)} %reshape.607, bf16[16,36,1024,1]{2,1,0,3:T(8,128)(2,1)S(1)} %reshape.606), kind=kOutput, calls=%fused_computation.74 | convolution fusion | flops 1061683200 | bytes 5096448 | tf_op jit(solution)/shard_map/xjf,clf->xjcl/dot_general | solution.py:105
  91.6 6.8 %fusion.28 = f32[16,36,25,36]{3,1,2,0:T(8,128)} fusion(bf16[25,36,1024,1]{2,1,0,3:T(8,128)(2,1)S(1)} %copy-done.14, bf16[16,36,1024,1]{2,1,0,3:T(8,128)(2,1)S(1)} %reshape.610), kind=kOutput, calls=%fused_computation.72 | convolution fusion | flops 1061683200 | bytes 5096448 | tf_op jit(solution)/shard_map/xjf,clf->xjcl/dot_general | solution.py:105
  100.1 8.8 %fusion.26 = f32[16,36,25,36]{3,1,2,0:T(8,128)} fusion(bf16[25,36,1024,1]{2,1,0,3:T(8,128)(2,1)} %reshape.607, bf16[16,36,1024,1]{2,1,0,3:T(8,128)(2,1)S(1)} %reshape.612), kind=kOutput, calls=%fused_computation.70 | convolution fusion | flops 1061683200 | bytes 5096448 | tf_op jit(solution)/shard_map/xjf,clf->xjcl/dot_general | solution.py:105
  111.8 6.7 %fusion.24 = f32[16,36,25,36]{3,1,2,0:T(8,128)S(1)} fusion(bf16[25,36,1024,1]{2,1,0,3:T(8,128)(2,1)} %reshape.607, bf16[16,36,1024,1]{2,1,0,3:T(8,128)(2,1)} %reshape.614), kind=kOutput, calls=%fused_computation.68 | convolution fusion | flops 1061683200 | bytes 5096448 | tf_op jit(solution)/shard_map/xjf,clf->xjcl/dot_general | solution.py:105
  118.5 4.6 %fusion.22 = f32[16,36,25,36]{3,1,2,0:T(8,128)S(1)} fusion(bf16[25,36,1024,1]{2,1,0,3:T(8,128)(2,1)S(1)} %copy-done.15, bf16[16,36,1024,1]{2,1,0,3:T(8,128)(2,1)S(1)} %copy-done.6), kind=kOutput, calls=%fused_computation.66 | convolution fusion | flops 1061683200 | bytes 5096448 | tf_op jit(solution)/shard_map/xjf,clf->xjcl/dot_general | solution.py:105
  123.2 5.4 %bitcast_dynamic-update-slice_fusion.4 = (f32[16,5,25,36]{3,2,0,1:T(8,128)}, f32[16,25,36]{2,1,0:T(8,128)}) fusion(s32[36,36]{1,0:T(8,128)S(1)} %add_select_fusion, f32[16,36,25,36]{3,1,2,0:T(8,128)S(1)} %bitcast.155), kind=kOutput, calls=%fused_computation.116 | convolution fusion | flops 224009856 | bytes 2603072 | tf_op jit(solution)/shard_map/xjcl,jlr->xcr/dot_general | solution.py:106
  128.6 5.6 %bitcast_dynamic-update-slice_fusion.3 = (f32[16,5,25,36]{3,2,0,1:T(8,128)}, f32[16,25,36]{2,1,0:T(8,128)}) fusion(f32[16,5,25,36]{3,2,0,1:T(8,128)} %get-tuple-element.62, s32[36,36]{1,0:T(8,128)S(1)} %add_select_fusion, f32[16,36,25,36]{3,1,2,0:T(8,128)S(1)} %bitcast.153), kind=kOutput, calls=%fused_computation.115 | convolution fusion | flops 224009856 | bytes 2603072 | tf_op jit(solution)/shard_map/xjcl,jlr->xcr/dot_general | solution.py:106
  134.2 5.4 %bitcast_dynamic-update-slice_fusion.2 = (f32[16,5,25,36]{3,2,0,1:T(8,128)}, f32[16,25,36]{2,1,0:T(8,128)}) fusion(f32[16,5,25,36]{3,2,0,1:T(8,128)} %get-tuple-element.64, s32[36,36]{1,0:T(8,128)S(1)} %add_select_fusion, f32[16,36,25,36]{3,1,2,0:T(8,128)S(1)} %bitcast.157), kind=kOutput, calls=%fused_computation.114 | convolution fusion | flops 224009856 | bytes 2603072 | tf_op jit(solution)/shard_map/xjcl,jlr->xcr/dot_general | solution.py:106
  139.6 5.8 %bitcast_dynamic-update-slice_fusion.1 = (f32[16,5,25,36]{3,2,0,1:T(8,128)}, f32[16,25,36]{2,1,0:T(8,128)}) fusion(f32[16,5,25,36]{3,2,0,1:T(8,128)} %get-tuple-element.66, s32[36,36]{1,0:T(8,128)S(1)} %add_select_fusion, f32[16,36,25,36]{3,1,2,0:T(8,128)S(1)} %fusion.24), kind=kOutput, calls=%fused_computation.113 | convolution fusion | flops 224009856 | bytes 2603072 | tf_op jit(solution)/shard_map/xjcl,jlr->xcr/dot_general | solution.py:106
  145.5 5.3 %bitcast_dynamic-update-slice_fusion = (f32[16,5,25,36]{3,2,0,1:T(8,128)}, f32[16,25,36]{2,1,0:T(8,128)S(1)}) fusion(f32[16,5,25,36]{3,2,0,1:T(8,128)} %get-tuple-element.68, s32[36,36]{1,0:T(8,128)S(1)} %add_select_fusion, f32[16,36,25,36]{3,1,2,0:T(8,128)S(1)} %fusion.22), kind=kOutput, calls=%fused_computation.112 | convolution fusion | flops 224009856 | bytes 2398528 | tf_op jit(solution)/shard_map/xjcl,jlr->xcr/dot_general | solution.py:106
  153.8 3.3 all-to-all-start.2
  157.8 4.5 %all-to-all-done.2 = f32[8,1,2]{2,1,0:T(1,128)S(1)} async-done(((f32[8,1,2]{2,1,0:T(1,128)}), f32[8,1,2]{2,1,0:T(1,128)S(1)}, u32[]{:S(2)}, u32[]{:S(2)}) %all-to-all-start.2) | async-done | bytes 96 | tf_op jit(solution)/shard_map/all_to_all | solution.py:119
  162.4 3.3 all-to-all-start.4
  165.8 5.1 %all-to-all-done.4 = f32[8,1,2]{2,1,0:T(1,128)S(1)} async-done(((f32[8,1,2]{2,1,0:T(1,128)}), f32[8,1,2]{2,1,0:T(1,128)S(1)}, u32[]{:S(2)}, u32[]{:S(2)}) %all-to-all-start.4) | async-done | bytes 96 | tf_op jit(solution)/shard_map/all_to_all | solution.py:122
  172.0 3.3 all-to-all-start.5
  176.0 4.5 %all-to-all-done.5 = f32[8,1,2]{2,1,0:T(1,128)S(1)} async-done(((f32[8,1,2]{2,1,0:T(1,128)}), f32[8,1,2]{2,1,0:T(1,128)S(1)}, u32[]{:S(2)}, u32[]{:S(2)}) %all-to-all-start.5) | async-done | bytes 96 | tf_op jit(solution)/shard_map/all_to_all | solution.py:134
  180.5 3.3 all-to-all-start.3
  185.3 3.7 all-to-all-done.3
  196.2 3.0 fusion.12
  200.7 3.3 fusion.14
  209.8 4.8 %bitcast_add_fusion = f32[25,36,1024]{2,1,0:T(8,128)S(1)} fusion(f32[25,36,1024,1]{2,1,3,0:T(8,128)S(1)} %fusion.10, f32[25,36,1024,1]{2,1,3,0:T(8,128)S(1)} %fusion.12, f32[25,36,1024,1]{2,1,3,0:T(8,128)S(1)} %fusion.14, f32[25,36,1024,1]{2,1,3,0:T(8,128)S(1)} %fusion.16, bf16[16,36,1024,1]{2,1,0,3:T(8,128)(2,1)} %copy-done.3, ...), kind=kOutput, calls=%fused_computation.12 | convolution fusion | flops 1065369600 | bytes 20648448 | tf_op jit(solution)/shard_map/xcjl,xjf->clf/dot_general | solution.py:150
  215.3 4.9 %copy.121 = f32[4,8,36,1024]{3,1,2,0:T(8,128)} copy(f32[4,8,36,1024]{3,2,1,0:T(8,128)S(1)} %bitcast.150) | data formatting | bytes 9437184
  220.2 74.4 %psum.15 = f32[25]{0:T(128)S(1)} all-reduce(f32[25]{0:T(128)S(1)} %add_add_fusion), channel_id=1, replica_groups=mesh['cls'=8,'dom'=32] {'dom'}, use_global_device_ids=true, to_apply=%region_17.18 | all-reduce | flops 25 | bytes 200 | tf_op jit(solution)/shard_map/psum | solution.py:154
  294.6 93.3 %all-reduce.2.cloned.1.call-done = f32[25,36864]{1,0:T(8,128)} async-done(((f32[25,36864]{1,0:T(8,128)}), f32[25,36864]{1,0:T(8,128)}) %all-reduce.2.cloned.1.call-update) | async-done | bytes 3686416 | tf_op jit(solution)/shard_map/psum | solution.py:154
  387.9 4.1 %divide_convert_fusion = bf16[25,36864]{1,0:T(8,128)(2,1)} fusion(f32[25,36864]{1,0:T(8,128)} %all-reduce.2.cloned.1.call-done, f32[25]{0:T(128)S(1)} %broadcast_add_fusion), kind=kLoop, calls=%fused_computation.11 | loop fusion | flops 1843200 | bytes 5529700 | tf_op jit(solution)/shard_map/convert_element_type | solution.py:155
  (128 shorter events, 45.8 us)
Async XLA Ops:
  6.5 7.0 %copy-start = (bf16[4,36864]{1,0:T(4,128)(2,1)S(1)}, bf16[4,36864]{1,0:T(4,128)(2,1)}, u32[]{:S(2)}) copy-start(bf16[4,36864]{1,0:T(4,128)(2,1)} %param.4) | copy-start | bytes 884740
  9.1 9.5 %all-to-all-start = ((bf16[8,2,16]{2,1,0:T(2,128)(2,1)}), bf16[8,2,16]{2,1,0:T(2,128)(2,1)S(1)}, u32[]{:S(2)}, u32[]{:S(2)}) async-start(bf16[8,2,16]{2,1,0:T(2,128)(2,1)} %copy.74), calls=%async_computation | async-start | bytes 8192 | tf_op jit(solution)/shard_map/all_to_all | solution.py:83
  18.6 21.1 %all-to-all-start.1 = ((bf16[8,2,36864]{2,1,0:T(2,128)(2,1)}), bf16[8,2,36864]{2,1,0:T(2,128)(2,1)S(1)}, u32[]{:S(2)}, u32[]{:S(2)}) async-start(bf16[8,2,36864]{2,1,0:T(2,128)(2,1)} %copy.75), calls=%async_computation.1 | async-start | bytes 2359296 | tf_op jit(solution)/shard_map/all_to_all | solution.py:82
  75.3 16.3 %copy-start.3 = (bf16[16,36,1024,1]{2,1,0,3:T(8,128)(2,1)}, bf16[16,36,1024,1]{2,1,0,3:T(8,128)(2,1)S(1)}, u32[]{:S(2)}) copy-start(bf16[16,36,1024,1]{2,1,0,3:T(8,128)(2,1)S(1)} %reshape.606) | copy-start | bytes 3538948
  82.2 9.4 %copy-start.4 = (bf16[16,36,1024,1]{2,1,0,3:T(8,128)(2,1)}, bf16[16,36,1024,1]{2,1,0,3:T(8,128)(2,1)S(1)}, u32[]{:S(2)}) copy-start(bf16[16,36,1024,1]{2,1,0,3:T(8,128)(2,1)S(1)} %reshape.610) | copy-start | bytes 3538948
  82.2 9.4 %copy-start.14 = (bf16[25,36,1024,1]{2,1,0,3:T(8,128)(2,1)S(1)}, bf16[25,36,1024,1]{2,1,0,3:T(8,128)(2,1)}, u32[]{:S(2)}) copy-start(bf16[25,36,1024,1]{2,1,0,3:T(8,128)(2,1)} %reshape.607) | copy-start | bytes 5529604
  91.6 6.8 %copy-start.12 = (bf16[16,144,1,128]{3,1,2,0:T(8,128)(2,1)S(1)}, bf16[16,144,1,128]{3,1,2,0:T(8,128)(2,1)}, u32[]{:S(2)}) copy-start(bf16[16,144,1,128]{3,1,2,0:T(8,128)(2,1)} %get-tuple-element.29) | copy-start | bytes 1769476
  91.6 6.8 %copy-start.13 = (bf16[16,144,1,128]{3,1,2,0:T(8,128)(2,1)S(1)}, bf16[16,144,1,128]{3,1,2,0:T(8,128)(2,1)}, u32[]{:S(2)}) copy-start(bf16[16,144,1,128]{3,1,2,0:T(8,128)(2,1)} %get-tuple-element.30) | copy-start | bytes 1769476
  100.1 8.9 %copy-start.8 = (bf16[16,36,1024,1]{2,1,0,3:T(8,128)(2,1)}, bf16[16,36,1024,1]{2,1,0,3:T(8,128)(2,1)S(1)}, u32[]{:S(2)}) copy-start(bf16[16,36,1024,1]{2,1,0,3:T(8,128)(2,1)S(1)} %reshape.612) | copy-start | bytes 3538948
  100.1 8.9 %copy-start.11 = (bf16[16,144,1,128]{3,1,2,0:T(8,128)(2,1)S(1)}, bf16[16,144,1,128]{3,1,2,0:T(8,128)(2,1)}, u32[]{:S(2)}) copy-start(bf16[16,144,1,128]{3,1,2,0:T(8,128)(2,1)} %get-tuple-element.38) | copy-start | bytes 1769476
  111.7 6.8 %copy-start.6 = (bf16[16,36,1024,1]{2,1,0,3:T(8,128)(2,1)S(1)}, bf16[16,36,1024,1]{2,1,0,3:T(8,128)(2,1)}, u32[]{:S(2)}) copy-start(bf16[16,36,1024,1]{2,1,0,3:T(8,128)(2,1)} %reshape.616) | copy-start | bytes 3538948
  111.7 6.8 %copy-start.15 = (bf16[25,36,1024,1]{2,1,0,3:T(8,128)(2,1)S(1)}, bf16[25,36,1024,1]{2,1,0,3:T(8,128)(2,1)}, u32[]{:S(2)}) copy-start(bf16[25,36,1024,1]{2,1,0,3:T(8,128)(2,1)} %reshape.607) | copy-start | bytes 5529604
  111.7 11.4 %slice-start.2 = ((s8[8192000]{0:T(1024)(128)(4,1)}), s8[4194304]{0:T(1024)(128)(4,1)S(1)}, s32[]{:S(2)}) async-start(s8[8192000]{0:T(1024)(128)(4,1)} %bitcast.154), calls=%async_computation.9 | async-start | bytes 8388608
  111.8 16.8 %slice-start = ((s8[8192000]{0:T(1024)(128)(4,1)}), s8[4194304]{0:T(1024)(128)(4,1)S(1)}, s32[]{:S(2)}) async-start(s8[8192000]{0:T(1024)(128)(4,1)} %bitcast.152), calls=%async_computation.7 | async-start | bytes 8388608
  118.5 4.6 %slice-start.3 = ((s8[8192000]{0:T(1024)(128)(4,1)}), s8[3997696]{0:T(1024)(128)(4,1)S(1)}, s32[]{:S(2)}) async-start(s8[8192000]{0:T(1024)(128)(4,1)} %bitcast.154), calls=%async_computation.10 | async-start | bytes 7995392
  118.5 10.1 %slice-start.1 = ((s8[8192000]{0:T(1024)(128)(4,1)}), s8[3997696]{0:T(1024)(128)(4,1)S(1)}, s32[]{:S(2)}) async-start(s8[8192000]{0:T(1024)(128)(4,1)} %bitcast.152), calls=%async_computation.8 | async-start | bytes 7995392
  123.1 11.1 %slice-start.4 = ((s8[8192000]{0:T(1024)(128)(4,1)}), s8[3997696]{0:T(1024)(128)(4,1)S(1)}, s32[]{:S(2)}) async-start(s8[8192000]{0:T(1024)(128)(4,1)} %bitcast.156), calls=%async_computation.11 | async-start | bytes 7995392
  128.6 5.6 %slice-start.5 = ((s8[8192000]{0:T(1024)(128)(4,1)}), s8[4194304]{0:T(1024)(128)(4,1)S(1)}, s32[]{:S(2)}) async-start(s8[8192000]{0:T(1024)(128)(4,1)} %bitcast.156), calls=%async_computation.12 | async-start | bytes 8388608
  150.8 2.6 copy-start.2
  150.8 39.0 %copy-start.16 = (f32[16,25,36]{2,1,0:T(8,128)S(1)}, f32[16,25,36]{2,1,0:T(8,128)}, u32[]{:S(2)}) copy-start(f32[16,25,36]{2,1,0:T(8,128)} %get-tuple-element.63) | copy-start | bytes 172804
  150.8 39.0 %copy-start.17 = (f32[16,25,36]{2,1,0:T(8,128)S(1)}, f32[16,25,36]{2,1,0:T(8,128)}, u32[]{:S(2)}) copy-start(f32[16,25,36]{2,1,0:T(8,128)} %get-tuple-element.65) | copy-start | bytes 172804
  150.8 39.0 %copy-start.18 = (f32[16,25,36]{2,1,0:T(8,128)S(1)}, f32[16,25,36]{2,1,0:T(8,128)}, u32[]{:S(2)}) copy-start(f32[16,25,36]{2,1,0:T(8,128)} %get-tuple-element.67) | copy-start | bytes 172804
  150.8 39.0 %copy-start.19 = (f32[16,25,36]{2,1,0:T(8,128)S(1)}, f32[16,25,36]{2,1,0:T(8,128)}, u32[]{:S(2)}) copy-start(f32[16,25,36]{2,1,0:T(8,128)} %get-tuple-element.69) | copy-start | bytes 172804
  153.8 8.6 %all-to-all-start.2 = ((f32[8,1,2]{2,1,0:T(1,128)}), f32[8,1,2]{2,1,0:T(1,128)S(1)}, u32[]{:S(2)}, u32[]{:S(2)}) async-start(f32[8,1,2]{2,1,0:T(1,128)} %bitcast.27), calls=%async_computation.2 | async-start | bytes 8192 | tf_op jit(solution)/shard_map/all_to_all | solution.py:119
  162.4 8.5 %all-to-all-start.4 = ((f32[8,1,2]{2,1,0:T(1,128)}), f32[8,1,2]{2,1,0:T(1,128)S(1)}, u32[]{:S(2)}, u32[]{:S(2)}) async-start(f32[8,1,2]{2,1,0:T(1,128)} %bitcast.30), calls=%async_computation.4 | async-start | bytes 8192 | tf_op jit(solution)/shard_map/all_to_all | solution.py:122
  172.0 8.5 %all-to-all-start.5 = ((f32[8,1,2]{2,1,0:T(1,128)}), f32[8,1,2]{2,1,0:T(1,128)S(1)}, u32[]{:S(2)}, u32[]{:S(2)}) async-start(f32[8,1,2]{2,1,0:T(1,128)} %copy.93), calls=%async_computation.5 | async-start | bytes 8192 | tf_op jit(solution)/shard_map/all_to_all | solution.py:134
  180.5 8.6 %all-to-all-start.3 = ((f32[8,1,2]{2,1,0:T(1,128)}), f32[8,1,2]{2,1,0:T(1,128)S(1)}, u32[]{:S(2)}, u32[]{:S(2)}) async-start(f32[8,1,2]{2,1,0:T(1,128)} %copy.90), calls=%async_computation.3 | async-start | bytes 8192 | tf_op jit(solution)/shard_map/all_to_all | solution.py:133
  183.8 204.1 %all-reduce.2.cloned.1.call-start = ((), (), s32[]{:S(2)}) async-start(), calls=%async_computation.6 | async-start | bytes 9437184 | tf_op jit(solution)/shard_map/psum | solution.py:154
  194.8 1.4 copy-start.10
  199.3 1.4 copy-start.9
  204.0 1.4 copy-start.5
  387.9 4.1 %copy-start.1 = (bf16[4,36864]{1,0:T(4,128)(2,1)S(1)}, bf16[4,36864]{1,0:T(4,128)(2,1)}, u32[]{:S(2)}) copy-start(bf16[4,36864]{1,0:T(4,128)(2,1)} %param.4) | copy-start | bytes 884740
  (1 other events, 1.4 us)
Sparse Core Ops, SparseCore 0:
  220.3 167.4 all-reduce.1
where the time goes:
time: 403 us; the launch traced here: 399 us
  waiting for transfers between devices  126 us (31%)
  matrix products  88.8 us (22%)
  blocking collectives  74.4 us (18%)
  other arithmetic  41.3 us (10%)
  local copies, waits for them, and re-layouts  32.9 us (8%)
  starting transfers between devices  21.7 us (5%)
  between operations  14.2 us (4%)
    psum x1, waiting for transfers between devices, shards(): summed, summed_mass = lax.psum((totals, masses), 'dom')  93.3 us
    psum x1, blocking collectives, shards(): summed, summed_mass = lax.psum((totals, masses), 'dom')  74.4 us
    dot_general x5, matrix products, shards(): jnp.einsum('xjf,clf->xjcl', moved, class_refs, preferred_element_type=jnp...  36.3 us
    add x2, other arithmetic, shift_images(): real_part * cosine + imag_part * sine  28.6 us
    dot_general x5, matrix products, shards(): jnp.einsum('xjcl,jlr->xcr', pairs, diagonal_f32, precision=lax.Precision....  27.6 us
    dot_general x5, matrix products, shards(): jnp.einsum('xcjl,xjf->clf', spread, moved_list[shift], preferred_element_...  17.1 us
    convert_element_type x10, local copies, waits for them, and re-layouts, shift_images(): return jnp.stack([real_part * cosine + imag_part * sine, imag_part * cosi...  13.4 us
    all_to_all x1, waiting for transfers between devices, shards(): lax.all_to_all(outgoing, 'cls', split_axis=0, concat_axis=0, tiled=True)  12.4 us
  transfers between devices with their start and end apart: 7, of which 7 were waited for; matrix products, arithmetic and copies ran while one was open for 2% of the time, Pallas kernels for 0%

commit v1 on v0

--- a/solution.py
+++ b/solution.py
@@ -3,13 +3,19 @@
 import jax
 import jax.numpy as jnp
 from jax import lax
+from jax.experimental import pallas as pl
+from jax.experimental.pallas import tpu as pltpu
 from jax.sharding import PartitionSpec as P
 
+MESH = pl.DeviceIdType.MESH
 CYCLES = 128
 ANGLES = 144
 ROT = 36
 SHIFTS = 5
 BOX = 256
+NCH, RC = 3, 80
+LEAD, DROWS = 15, 225
+CLS_LOC, ROTS = 25, 36
 
 
 SOFTMAX_WARMTH = 2.0
@@ -37,6 +43,123 @@
     return jnp.stack(
         [real_part * cosine + imag_part * sine, imag_part * cosine - real_part * sine], axis=-2
     ).astype(jnp.bfloat16)
+
+
+def reduce_kernel(p_ref, g_ref, x1, x2, d3, d4, e5, e6, c1, c2, s_buf, z_buf, ysend, yrecv, zsend, zrecv):
+    dom = lax.axis_index("dom")
+    y = dom % 4
+    z = dom // 4
+    yp, ym, yo = (y + 1) % 4, (y + 3) % 4, (y + 2) % 4
+    up, down = {"dom": z * 4 + yp}, {"dom": z * 4 + ym}
+    zdev = [{"dom": ((z + k) % 8) * 4 + y} for k in range(8)]
+    barrier = pltpu.get_barrier_semaphore()
+    for target in [up, down] + zdev[1:]:
+        pl.semaphore_signal(barrier, inc=1, device_id=target, device_id_type=MESH)
+    pl.semaphore_wait(barrier, 9)
+    A, B = pl.ds(0, 4), pl.ds(4, 4)
+
+    def send(src, dst, ssem, rsem, target):
+        copy = pltpu.make_async_remote_copy(src_ref=src, dst_ref=dst, send_sem=ssem, recv_sem=rsem,
+                                            device_id=target, device_id_type=MESH)
+        copy.start()
+        return copy
+
+    pending = []
+    m1, m2, m3, m4, m5, m6 = {}, {}, {}, {}, {}, {}
+    for ch in range(NCH):
+        m1[ch] = send(p_ref.at[ch, yo, A], x1.at[ch], ysend.at[ch, 0], yrecv.at[ch, 0], up)
+        m2[ch] = send(p_ref.at[ch, yo, B], x2.at[ch], ysend.at[ch, 1], yrecv.at[ch, 1], down)
+        m3[ch] = send(p_ref.at[ch, yp, B], d3.at[ch], ysend.at[ch, 2], yrecv.at[ch, 2], up)
+        m4[ch] = send(p_ref.at[ch, ym, A], d4.at[ch], ysend.at[ch, 3], yrecv.at[ch, 3], down)
+    for ch in range(NCH):
+        m1[ch].wait_recv()
+        c1[ch] = (x1[ch].astype(jnp.float32) + p_ref[ch, yp, A].astype(jnp.float32)).astype(jnp.bfloat16)
+        m5[ch] = send(c1.at[ch], e5.at[ch], ysend.at[ch, 4], yrecv.at[ch, 4], up)
+        m2[ch].wait_recv()
+        c2[ch] = (x2[ch].astype(jnp.float32) + p_ref[ch, ym, B].astype(jnp.float32)).astype(jnp.bfloat16)
+        m6[ch] = send(c2.at[ch], e6.at[ch], ysend.at[ch, 5], yrecv.at[ch, 5], down)
+    zm = {}
+    for ch in range(NCH):
+        m4[ch].wait_recv()
+        m5[ch].wait_recv()
+        s_buf[ch, A] = (p_ref[ch, y, A].astype(jnp.float32) + e5[ch].astype(jnp.float32)
+                        + d4[ch].astype(jnp.float32)).astype(jnp.bfloat16)
+        m3[ch].wait_recv()
+        m6[ch].wait_recv()
+        s_buf[ch, B] = (p_ref[ch, y, B].astype(jnp.float32) + e6[ch].astype(jnp.float32)
+                        + d3[ch].astype(jnp.float32)).astype(jnp.bfloat16)
+        for k in range(1, 8):
+            zm[ch, k] = send(s_buf.at[ch, (z + k) % 8], z_buf.at[ch, k - 1],
+                             zsend.at[ch, k - 1], zrecv.at[ch, k - 1], zdev[k])
+    zg = {}
+    mass = None
+    for ch in range(NCH):
+        num = s_buf[ch, z].astype(jnp.float32)
+        for k in range(1, 8):
+            zm[ch, k].wait_recv()
+            num = num + z_buf[ch, k - 1].astype(jnp.float32)
+        if ch == 0:
+            mass = num[0:1, :] + num[1:2, :] + 1.0
+        place = DROWS * y + (ch * RC - LEAD) + lax.broadcasted_iota(jnp.int32, (RC, 128), 0)
+        den = jnp.ones((RC, 128), jnp.float32)
+        for c in range(CLS_LOC):
+            here = (place >= c * ROTS) & (place < (c + 1) * ROTS)
+            den = jnp.where(here, jnp.broadcast_to(mass[:, c:c + 1], (RC, 128)), den)
+        g_ref[ch, y, z] = (num / den).astype(jnp.bfloat16)
+        for k in range(1, 8):
+            zg[ch, k] = send(g_ref.at[ch, y, z], g_ref.at[ch, y, z],
+                             zsend.at[ch, 6 + k], zrecv.at[ch, 6 + k], zdev[k])
+    m7, m8, m9, m10 = {}, {}, {}, {}
+    for ch in range(NCH):
+        for k in range(1, 8):
+            zg[ch, k].wait_recv()
+        m7[ch] = send(g_ref.at[ch, y], g_ref.at[ch, y], ysend.at[ch, 6], yrecv.at[ch, 6], up)
+        m8[ch] = send(g_ref.at[ch, y], g_ref.at[ch, y], ysend.at[ch, 7], yrecv.at[ch, 7], down)
+    for ch in range(NCH):
+        m7[ch].wait_recv()
+        m9[ch] = send(g_ref.at[ch, ym, A], g_ref.at[ch, ym, A], ysend.at[ch, 8], yrecv.at[ch, 8], up)
+        m8[ch].wait_recv()
+        m10[ch] = send(g_ref.at[ch, yp, B], g_ref.at[ch, yp, B], ysend.at[ch, 9], yrecv.at[ch, 9], down)
+    for ch in range(NCH):
+        m9[ch].wait_recv()
+        m10[ch].wait_recv()
+    for group in (m1, m2, m3, m4, m5, m6, zm, zg, m7, m8, m9, m10):
+        for copy in group.values():
+            copy.wait_send()
+
+
+def reduce_average(payload):
+    half = pltpu.VMEM((NCH, 4, RC, 128), jnp.bfloat16)
+    return pl.pallas_call(
+        reduce_kernel,
+        out_shape=jax.ShapeDtypeStruct((NCH, 4, 8, RC, 128), jnp.bfloat16),
+        in_specs=[pl.BlockSpec(memory_space=pltpu.VMEM)],
+        out_specs=pl.BlockSpec(memory_space=pltpu.VMEM),
+        scratch_shapes=[half] * 8 + [
+            pltpu.VMEM((NCH, 8, RC, 128), jnp.bfloat16),
+            pltpu.VMEM((NCH, 7, RC, 128), jnp.bfloat16),
+            pltpu.SemaphoreType.DMA((NCH, 10)),
+            pltpu.SemaphoreType.DMA((NCH, 10)),
+            pltpu.SemaphoreType.DMA((NCH, 14)),
+            pltpu.SemaphoreType.DMA((NCH, 14)),
+        ],
+        compiler_params=pltpu.CompilerParams(collective_id=5, has_side_effects=True, vmem_limit_bytes=40 << 20),
+        name="reduce_average",
+    )(payload)
+
+
+def pack_payload(totals, masses):
+    rows = totals.reshape(4, DROWS, 8, 128)
+    hi = masses.astype(jnp.bfloat16).astype(jnp.float32)
+    lead = jnp.pad(jnp.stack([hi, masses - hi]), ((0, LEAD - 2), (0, 128 - CLS_LOC)))
+    lead = jnp.broadcast_to(lead[None, :, None, :], (4, LEAD, 8, 128))
+    whole = jnp.concatenate([lead, rows], axis=1).astype(jnp.bfloat16)
+    return whole.reshape(4, NCH, RC, 8, 128).transpose(1, 0, 3, 2, 4)
+
+
+def unpack_average(gathered):
+    rows = gathered.transpose(1, 0, 3, 2, 4).reshape(4, NCH * RC, 8, 128)[:, LEAD:]
+    return rows.reshape(CLS_LOC, 36864)
 
 
 def shards(particles, references, candidates, offsets):
@@ -150,9 +273,7 @@
         totals = totals + jnp.einsum(
             "xcjl,xjf->clf", spread, moved_list[shift], preferred_element_type=jnp.float32
         )
-    totals = totals.reshape(local, width)
-    summed, summed_mass = lax.psum((totals, masses), "dom")
-    return (summed / (summed_mass + PRIOR_MASS)[:, None]).astype(jnp.bfloat16)
+    return unpack_average(reduce_average(pack_payload(totals, masses)))
 
 
 def solution(mesh):

time: 403 us -> 277 us (0.69)
  waiting for transfers between devices: 126 us -> 32.4 us
  blocking collectives: 74.4 us -> 0 us
  Pallas kernels: 0 us -> 58.1 us
  between operations: 14.2 us -> 0.87 us
    psum x1 -> x0, waiting for transfers between devices: 93.3 us -> none  [shards(): summed, summed_mass = lax.psum((totals, masses), 'dom')]
    psum x1 -> x0, blocking collectives: 74.4 us -> none  [shards(): summed, summed_mass = lax.psum((totals, masses), 'dom')]
    pallas_call x0 -> x1, Pallas kernels: none -> 58.1 us  [reduce_average(): pl.pallas_call(reduce_kernel, out_shape=jax.ShapeDtypeStruct((NCH, 4, 8,...]
    unnamed x55 -> x53, local copies, waits for them, and re-layouts: 6.41 us -> 0.88 us
    reshape x0 -> x2, local copies, waits for them, and re-layouts: none -> 4.41 us  [the longest x1 2.24 us: unpack_average(): return rows.reshape(CLS_LOC, 36864)]
    convert_element_type x1, other arithmetic: 4.13 us -> 0.01 us  [pack_payload(): hi = masses.astype(jnp.bfloat16).astype(jnp.float32)]
  transfers between devices with their start and end apart: 7 -> 6, of which waited for: 7 -> 6; matrix products, arithmetic and copies ran while one was open for 2% -> 4% of each run, Pallas kernels for 0% -> 0%
where the time goes in v1:
time: 277 us; the launch traced here: 274 us
  matrix products  88.8 us (32%)
  Pallas kernels  58.1 us (21%)
  other arithmetic  38.9 us (14%)
  local copies, waits for them, and re-layouts  33.1 us (12%)
  waiting for transfers between devices  32.4 us (12%)
  starting transfers between devices  21.8 us (8%)
    pallas_call x1, Pallas kernels, reduce_average(): pl.pallas_call(reduce_kernel, out_shape=jax.ShapeDtypeStruct((NCH, 4, 8,...  58.1 us
    dot_general x5, matrix products, shards(): jnp.einsum('xjf,clf->xjcl', moved, class_refs, preferred_element_type=jnp...  36.1 us
    add x2, other arithmetic, shift_images(): real_part * cosine + imag_part * sine  28.6 us
    dot_general x5, matrix products, shards(): jnp.einsum('xjcl,jlr->xcr', pairs, diagonal_f32, precision=lax.Precision....  27.4 us
    dot_general x5, matrix products, shards(): jnp.einsum('xcjl,xjf->clf', spread, moved_list[shift], preferred_element_...  17.6 us
    convert_element_type x10, local copies, waits for them, and re-layouts, shift_images(): return jnp.stack([real_part * cosine + imag_part * sine, imag_part * cosi...  13.7 us
    all_to_all x1, waiting for transfers between devices, shards(): lax.all_to_all(outgoing, 'cls', split_axis=0, concat_axis=0, tiled=True)  12.4 us
    dot_general x5, matrix products, shards(): jnp.einsum('xcr,jlr->xcjl', weight, diagonal_bf16, preferred_element_type...  7.05 us
  transfers between devices with their start and end apart: 6, of which 6 were waited for; matrix products, arithmetic and copies ran while one was open for 4% of the time, Pallas kernels for 0%

profile of v1, /device:TPU:8, one launch (start us, length us, event | category | flops | bytes accessed | tf_op | source)
XLA Modules:
  0.0 273.9 jit_solution(13170994898837738797)
XLA Ops:
  2.6 4.3 %all-to-all-start = ((bf16[8,2,16]{2,1,0:T(2,128)(2,1)}), bf16[8,2,16]{2,1,0:T(2,128)(2,1)S(1)}, u32[]{:S(2)}, u32[]{:S(2)}) async-start(bf16[8,2,16]{2,1,0:T(2,128)(2,1)} %copy.82), calls=%async_computation | async-start | bytes 8192 | tf_op jit(solution)/shard_map/all_to_all | solution.py:206
  9.7 2.4 all-to-all-done
  12.1 3.8 %all-to-all-start.1 = ((bf16[8,2,36864]{2,1,0:T(2,128)(2,1)}), bf16[8,2,36864]{2,1,0:T(2,128)(2,1)S(1)}, u32[]{:S(2)}, u32[]{:S(2)}) async-start(bf16[8,2,36864]{2,1,0:T(2,128)(2,1)} %copy.83), calls=%async_computation.1 | async-start | bytes 2359296 | tf_op jit(solution)/shard_map/all_to_all | solution.py:205
  15.9 4.1 %reshape.684 = bf16[25,36,1024,1]{2,1,0,3:T(8,128)(2,1)} reshape(bf16[25,36864]{1,0:T(8,128)(2,1)} %param.5) | data formatting | bytes 3686400 | tf_op jit(solution)/shard_map/reshape | solution.py:221
  20.7 12.4 %all-to-all-done.1 = bf16[8,2,36864]{2,1,0:T(2,128)(2,1)S(1)} async-done(((bf16[8,2,36864]{2,1,0:T(2,128)(2,1)}), bf16[8,2,36864]{2,1,0:T(2,128)(2,1)S(1)}, u32[]{:S(2)}, u32[]{:S(2)}) %all-to-all-start.1) | async-done | bytes 1179680 | tf_op jit(solution)/shard_map/all_to_all | solution.py:205
  35.7 4.9 %fusion.39 = (bf16[16,144,1,128]{3,1,2,0:T(8,128)(2,1)S(1)}, bf16[16,144,1,128]{3,1,2,0:T(8,128)(2,1)S(1)}, bf16[16,144,1,128]{3,1,2,0:T(8,128)(2,1)S(1)}) fusion(f32[16,144]{1,0:T(8,128)S(1)} %get-tuple-element.60, f32[128]{0:T(128)S(1)} %iota_add_fusion, bf16[16,144,1,128]{3,2,1,0:T(2,128)(2,1)S(1)} %get-tuple-element.48, ...), kind=kLoop, calls=%fused_computation.86 | loop fusion | flops 2064384 | bytes 2958848 | tf_op jit(solution)/shard_map/add | solution.py:44
  40.7 23.6 %fusion.37 = (bf16[16,144,1,128]{3,1,2,0:T(8,128)(2,1)}, bf16[16,144,1,128]{3,1,2,0:T(8,128)(2,1)}, bf16[16,144,1,128]{3,1,2,0:T(8,128)(2,1)}, bf16[16,144,1,128...) fusion(bf16[16,144,1,128]{3,1,2,0:T(8,128)(2,1)S(1)} %get-tuple, ...), kind=kLoop, calls=%fused_computation.84 | loop fusion | flops 12681216 | bytes 6534656 | tf_op jit(solution)/shard_map/add | solution.py:44
  72.4 3.1 %reshape.687 = bf16[16,36,1024,1]{2,1,0,3:T(8,128)(2,1)S(1)} reshape(bf16[16,144,2,128]{3,2,1,0:T(2,128)(2,1)} %copy.88) | data formatting | bytes 2359296 | tf_op jit(solution)/shard_map/convert_element_type | solution.py:45
  75.6 9.2 %fusion.31 = f32[16,36,25,36]{3,1,2,0:T(8,128)} fusion(bf16[25,36,1024,1]{2,1,0,3:T(8,128)(2,1)} %reshape.684, bf16[16,36,1024,1]{2,1,0,3:T(8,128)(2,1)S(1)} %reshape.683), kind=kOutput, calls=%fused_computation.76 | convolution fusion | flops 1061683200 | bytes 5096448 | tf_op jit(solution)/shard_map/xjf,clf->xjcl/dot_general | solution.py:228
  84.8 6.8 %fusion.29 = f32[16,36,25,36]{3,1,2,0:T(8,128)} fusion(bf16[25,36,1024,1]{2,1,0,3:T(8,128)(2,1)S(1)} %copy-done.14, bf16[16,36,1024,1]{2,1,0,3:T(8,128)(2,1)S(1)} %reshape.687), kind=kOutput, calls=%fused_computation.74 | convolution fusion | flops 1061683200 | bytes 5096448 | tf_op jit(solution)/shard_map/xjf,clf->xjcl/dot_general | solution.py:228
  93.3 8.8 %fusion.27 = f32[16,36,25,36]{3,1,2,0:T(8,128)} fusion(bf16[25,36,1024,1]{2,1,0,3:T(8,128)(2,1)} %reshape.684, bf16[16,36,1024,1]{2,1,0,3:T(8,128)(2,1)S(1)} %reshape.689), kind=kOutput, calls=%fused_computation.72 | convolution fusion | flops 1061683200 | bytes 5096448 | tf_op jit(solution)/shard_map/xjf,clf->xjcl/dot_general | solution.py:228
  105.3 6.7 %fusion.25 = f32[16,36,25,36]{3,1,2,0:T(8,128)S(1)} fusion(bf16[25,36,1024,1]{2,1,0,3:T(8,128)(2,1)} %reshape.684, bf16[16,36,1024,1]{2,1,0,3:T(8,128)(2,1)} %reshape.691), kind=kOutput, calls=%fused_computation.70 | convolution fusion | flops 1061683200 | bytes 5096448 | tf_op jit(solution)/shard_map/xjf,clf->xjcl/dot_general | solution.py:228
  112.0 4.6 %fusion.23 = f32[16,36,25,36]{3,1,2,0:T(8,128)S(1)} fusion(bf16[25,36,1024,1]{2,1,0,3:T(8,128)(2,1)S(1)} %copy-done.15, bf16[16,36,1024,1]{2,1,0,3:T(8,128)(2,1)S(1)} %copy-done.6), kind=kOutput, calls=%fused_computation.68 | convolution fusion | flops 1061683200 | bytes 5096448 | tf_op jit(solution)/shard_map/xjf,clf->xjcl/dot_general | solution.py:228
  116.6 5.4 %bitcast_dynamic-update-slice_fusion.4 = (f32[16,5,25,36]{3,2,0,1:T(8,128)}, f32[16,25,36]{2,1,0:T(8,128)}) fusion(s32[36,36]{1,0:T(8,128)S(1)} %add_select_fusion, f32[16,36,25,36]{3,1,2,0:T(8,128)S(1)} %bitcast.169), kind=kOutput, calls=%fused_computation.118 | convolution fusion | flops 224009856 | bytes 2603072 | tf_op jit(solution)/shard_map/xjcl,jlr->xcr/dot_general | solution.py:229
  122.1 5.6 %bitcast_dynamic-update-slice_fusion.3 = (f32[16,5,25,36]{3,2,0,1:T(8,128)}, f32[16,25,36]{2,1,0:T(8,128)}) fusion(f32[16,5,25,36]{3,2,0,1:T(8,128)} %get-tuple-element.64, s32[36,36]{1,0:T(8,128)S(1)} %add_select_fusion, f32[16,36,25,36]{3,1,2,0:T(8,128)S(1)} %bitcast.167), kind=kOutput, calls=%fused_computation.117 | convolution fusion | flops 224009856 | bytes 2603072 | tf_op jit(solution)/shard_map/xjcl,jlr->xcr/dot_general | solution.py:229
  127.7 5.4 %bitcast_dynamic-update-slice_fusion.2 = (f32[16,5,25,36]{3,2,0,1:T(8,128)}, f32[16,25,36]{2,1,0:T(8,128)}) fusion(f32[16,5,25,36]{3,2,0,1:T(8,128)} %get-tuple-element.66, s32[36,36]{1,0:T(8,128)S(1)} %add_select_fusion, f32[16,36,25,36]{3,1,2,0:T(8,128)S(1)} %bitcast.171), kind=kOutput, calls=%fused_computation.116 | convolution fusion | flops 224009856 | bytes 2603072 | tf_op jit(solution)/shard_map/xjcl,jlr->xcr/dot_general | solution.py:229
  133.1 5.6 %bitcast_dynamic-update-slice_fusion.1 = (f32[16,5,25,36]{3,2,0,1:T(8,128)}, f32[16,25,36]{2,1,0:T(8,128)}) fusion(f32[16,5,25,36]{3,2,0,1:T(8,128)} %get-tuple-element.68, s32[36,36]{1,0:T(8,128)S(1)} %add_select_fusion, f32[16,36,25,36]{3,1,2,0:T(8,128)S(1)} %fusion.25), kind=kOutput, calls=%fused_computation.115 | convolution fusion | flops 224009856 | bytes 2603072 | tf_op jit(solution)/shard_map/xjcl,jlr->xcr/dot_general | solution.py:229
  138.7 5.3 %bitcast_dynamic-update-slice_fusion = (f32[16,5,25,36]{3,2,0,1:T(8,128)}, f32[16,25,36]{2,1,0:T(8,128)S(1)}) fusion(f32[16,5,25,36]{3,2,0,1:T(8,128)} %get-tuple-element.70, s32[36,36]{1,0:T(8,128)S(1)} %add_select_fusion, f32[16,36,25,36]{3,1,2,0:T(8,128)S(1)} %fusion.23), kind=kOutput, calls=%fused_computation.114 | convolution fusion | flops 224009856 | bytes 2398528 | tf_op jit(solution)/shard_map/xjcl,jlr->xcr/dot_general | solution.py:229
  147.1 3.3 %all-to-all-start.2 = ((f32[8,1,2]{2,1,0:T(1,128)}), f32[8,1,2]{2,1,0:T(1,128)S(1)}, u32[]{:S(2)}, u32[]{:S(2)}) async-start(f32[8,1,2]{2,1,0:T(1,128)} %bitcast.27), calls=%async_computation.2 | async-start | bytes 8192 | tf_op jit(solution)/shard_map/all_to_all | solution.py:242
  151.1 4.5 %all-to-all-done.2 = f32[8,1,2]{2,1,0:T(1,128)S(1)} async-done(((f32[8,1,2]{2,1,0:T(1,128)}), f32[8,1,2]{2,1,0:T(1,128)S(1)}, u32[]{:S(2)}, u32[]{:S(2)}) %all-to-all-start.2) | async-done | bytes 96 | tf_op jit(solution)/shard_map/all_to_all | solution.py:242
  155.6 3.3 %all-to-all-start.4 = ((f32[8,1,2]{2,1,0:T(1,128)}), f32[8,1,2]{2,1,0:T(1,128)S(1)}, u32[]{:S(2)}, u32[]{:S(2)}) async-start(f32[8,1,2]{2,1,0:T(1,128)} %bitcast.30), calls=%async_computation.4 | async-start | bytes 8192 | tf_op jit(solution)/shard_map/all_to_all | solution.py:245
  159.0 5.1 %all-to-all-done.4 = f32[8,1,2]{2,1,0:T(1,128)S(1)} async-done(((f32[8,1,2]{2,1,0:T(1,128)}), f32[8,1,2]{2,1,0:T(1,128)S(1)}, u32[]{:S(2)}, u32[]{:S(2)}) %all-to-all-start.4) | async-done | bytes 96 | tf_op jit(solution)/shard_map/all_to_all | solution.py:245
  165.3 3.3 %all-to-all-start.5 = ((f32[8,1,2]{2,1,0:T(1,128)}), f32[8,1,2]{2,1,0:T(1,128)S(1)}, u32[]{:S(2)}, u32[]{:S(2)}) async-start(f32[8,1,2]{2,1,0:T(1,128)} %copy.101), calls=%async_computation.5 | async-start | bytes 8192 | tf_op jit(solution)/shard_map/all_to_all | solution.py:257
  169.3 4.5 %all-to-all-done.5 = f32[8,1,2]{2,1,0:T(1,128)S(1)} async-done(((f32[8,1,2]{2,1,0:T(1,128)}), f32[8,1,2]{2,1,0:T(1,128)S(1)}, u32[]{:S(2)}, u32[]{:S(2)}) %all-to-all-start.5) | async-done | bytes 96 | tf_op jit(solution)/shard_map/all_to_all | solution.py:257
  173.7 3.7 %all-to-all-start.3 = ((f32[8,1,2]{2,1,0:T(1,128)}), f32[8,1,2]{2,1,0:T(1,128)S(1)}, u32[]{:S(2)}, u32[]{:S(2)}) async-start(f32[8,1,2]{2,1,0:T(1,128)} %copy.98), calls=%async_computation.3 | async-start | bytes 8192 | tf_op jit(solution)/shard_map/all_to_all | solution.py:256
  178.7 3.5 %all-to-all-done.3 = f32[8,1,2]{2,1,0:T(1,128)S(1)} async-done(((f32[8,1,2]{2,1,0:T(1,128)}), f32[8,1,2]{2,1,0:T(1,128)S(1)}, u32[]{:S(2)}, u32[]{:S(2)}) %all-to-all-start.3) | async-done | bytes 96 | tf_op jit(solution)/shard_map/all_to_all | solution.py:256
  185.0 3.0 %fusion.11 = f32[25,36,1024,1]{2,1,3,0:T(8,128)S(1)} fusion(bf16[16,36,1024,1]{2,1,0,3:T(8,128)(2,1)S(1)} %copy-done.7, bf16[16,25,36,36]{3,1,2,0:T(8,128)(2,1)S(1)} %convolution_convert_fusion.1), kind=kOutput, calls=%fused_computation.16 | convolution fusion | flops 1061683200 | bytes 5902848 | tf_op jit(solution)/shard_map/xcjl,xjf->clf/dot_general | solution.py:273
  189.5 3.0 %fusion.13 = f32[25,36,1024,1]{2,1,3,0:T(8,128)S(1)} fusion(bf16[16,36,1024,1]{2,1,0,3:T(8,128)(2,1)S(1)} %copy-done.10, bf16[16,25,36,36]{3,1,2,0:T(8,128)(2,1)S(1)} %convolution_convert_fusion.2), kind=kOutput, calls=%fused_computation.18 | convolution fusion | flops 1061683200 | bytes 5902848 | tf_op jit(solution)/shard_map/xcjl,xjf->clf/dot_general | solution.py:273
  194.0 3.2 %fusion.15 = f32[25,36,1024,1]{2,1,3,0:T(8,128)S(1)} fusion(bf16[16,36,1024,1]{2,1,0,3:T(8,128)(2,1)S(1)} %copy-done.9, bf16[16,25,36,36]{3,1,2,0:T(8,128)(2,1)S(1)} %convolution_convert_fusion.3), kind=kOutput, calls=%fused_computation.20 | convolution fusion | flops 1061683200 | bytes 5902848 | tf_op jit(solution)/shard_map/xcjl,xjf->clf/dot_general | solution.py:273
  198.6 3.0 %fusion.17 = f32[25,36,1024,1]{2,1,3,0:T(8,128)S(1)} fusion(bf16[16,36,1024,1]{2,1,0,3:T(8,128)(2,1)S(1)} %copy-done.5, bf16[16,25,36,36]{3,1,2,0:T(8,128)(2,1)S(1)} %convolution_convert_fusion.4), kind=kOutput, calls=%fused_computation.22 | convolution fusion | flops 1061683200 | bytes 5902848 | tf_op jit(solution)/shard_map/xcjl,xjf->clf/dot_general | solution.py:273
  203.1 5.3 %fusion.10 = bf16[25,36,1024]{2,1,0:T(8,128)(2,1)S(1)} fusion(f32[25,36,1024,1]{2,1,3,0:T(8,128)S(1)} %fusion.11, f32[25,36,1024,1]{2,1,3,0:T(8,128)S(1)} %fusion.13, f32[25,36,1024,1]{2,1,3,0:T(8,128)S(1)} %fusion.15, f32[25,36,1024,1]{2,1,3,0:T(8,128)S(1)} %fusion.17, bf16[16,36,1024,1]{2,1,0,3:T(8,128)(2,1)} %copy-done.3, ...), kind=kOutput, calls=%fused_computation.12 | convolution fusion | flops 1066291200 | bytes 18805248 | tf_op jit(solution)/shard_map/xcjl,xjf->clf/dot_general | solution.py:273
  212.7 58.1 %reduce_average.1 = bf16[3,4,8,80,128]{4,3,2,1,0:T(8,128)(2,1)S(1)} custom-call(bf16[3,4,8,80,128]{4,3,2,1,0:T(8,128)(2,1)S(1)} %bitcast.164), custom_call_target="tpu_custom_call" | custom-call | tf_op jit(solution)/shard_map/reduce_average/pallas_call | solution.py:133
  (130 shorter events, 43.9 us)
Async XLA Ops:
  0.0 7.0 %copy-start = (bf16[4,36864]{1,0:T(4,128)(2,1)S(1)}, bf16[4,36864]{1,0:T(4,128)(2,1)}, u32[]{:S(2)}) copy-start(bf16[4,36864]{1,0:T(4,128)(2,1)} %param.4) | copy-start | bytes 884740
  2.6 9.5 %all-to-all-start = ((bf16[8,2,16]{2,1,0:T(2,128)(2,1)}), bf16[8,2,16]{2,1,0:T(2,128)(2,1)S(1)}, u32[]{:S(2)}, u32[]{:S(2)}) async-start(bf16[8,2,16]{2,1,0:T(2,128)(2,1)} %copy.82), calls=%async_computation | async-start | bytes 8192 | tf_op jit(solution)/shard_map/all_to_all | solution.py:206
  12.1 21.0 %all-to-all-start.1 = ((bf16[8,2,36864]{2,1,0:T(2,128)(2,1)}), bf16[8,2,36864]{2,1,0:T(2,128)(2,1)S(1)}, u32[]{:S(2)}, u32[]{:S(2)}) async-start(bf16[8,2,36864]{2,1,0:T(2,128)(2,1)} %copy.83), calls=%async_computation.1 | async-start | bytes 2359296 | tf_op jit(solution)/shard_map/all_to_all | solution.py:205
  68.6 16.1 %copy-start.3 = (bf16[16,36,1024,1]{2,1,0,3:T(8,128)(2,1)}, bf16[16,36,1024,1]{2,1,0,3:T(8,128)(2,1)S(1)}, u32[]{:S(2)}) copy-start(bf16[16,36,1024,1]{2,1,0,3:T(8,128)(2,1)S(1)} %reshape.683) | copy-start | bytes 3538948
  75.6 9.2 %copy-start.4 = (bf16[16,36,1024,1]{2,1,0,3:T(8,128)(2,1)}, bf16[16,36,1024,1]{2,1,0,3:T(8,128)(2,1)S(1)}, u32[]{:S(2)}) copy-start(bf16[16,36,1024,1]{2,1,0,3:T(8,128)(2,1)S(1)} %reshape.687) | copy-start | bytes 3538948
  75.6 9.2 %copy-start.14 = (bf16[25,36,1024,1]{2,1,0,3:T(8,128)(2,1)S(1)}, bf16[25,36,1024,1]{2,1,0,3:T(8,128)(2,1)}, u32[]{:S(2)}) copy-start(bf16[25,36,1024,1]{2,1,0,3:T(8,128)(2,1)} %reshape.684) | copy-start | bytes 5529604
  84.8 6.8 %copy-start.12 = (bf16[16,144,1,128]{3,1,2,0:T(8,128)(2,1)S(1)}, bf16[16,144,1,128]{3,1,2,0:T(8,128)(2,1)}, u32[]{:S(2)}) copy-start(bf16[16,144,1,128]{3,1,2,0:T(8,128)(2,1)} %get-tuple-element.31) | copy-start | bytes 1769476
  84.8 6.8 %copy-start.13 = (bf16[16,144,1,128]{3,1,2,0:T(8,128)(2,1)S(1)}, bf16[16,144,1,128]{3,1,2,0:T(8,128)(2,1)}, u32[]{:S(2)}) copy-start(bf16[16,144,1,128]{3,1,2,0:T(8,128)(2,1)} %get-tuple-element.32) | copy-start | bytes 1769476
  93.3 8.9 %copy-start.8 = (bf16[16,36,1024,1]{2,1,0,3:T(8,128)(2,1)}, bf16[16,36,1024,1]{2,1,0,3:T(8,128)(2,1)S(1)}, u32[]{:S(2)}) copy-start(bf16[16,36,1024,1]{2,1,0,3:T(8,128)(2,1)S(1)} %reshape.689) | copy-start | bytes 3538948
  93.3 8.9 %copy-start.11 = (bf16[16,144,1,128]{3,1,2,0:T(8,128)(2,1)S(1)}, bf16[16,144,1,128]{3,1,2,0:T(8,128)(2,1)}, u32[]{:S(2)}) copy-start(bf16[16,144,1,128]{3,1,2,0:T(8,128)(2,1)} %get-tuple-element.40) | copy-start | bytes 1769476
  105.2 6.8 %copy-start.6 = (bf16[16,36,1024,1]{2,1,0,3:T(8,128)(2,1)S(1)}, bf16[16,36,1024,1]{2,1,0,3:T(8,128)(2,1)}, u32[]{:S(2)}) copy-start(bf16[16,36,1024,1]{2,1,0,3:T(8,128)(2,1)} %reshape.693) | copy-start | bytes 3538948
  105.2 6.8 %copy-start.15 = (bf16[25,36,1024,1]{2,1,0,3:T(8,128)(2,1)S(1)}, bf16[25,36,1024,1]{2,1,0,3:T(8,128)(2,1)}, u32[]{:S(2)}) copy-start(bf16[25,36,1024,1]{2,1,0,3:T(8,128)(2,1)} %reshape.684) | copy-start | bytes 5529604
  105.2 11.4 %slice-start.2 = ((s8[8192000]{0:T(1024)(128)(4,1)}), s8[4194304]{0:T(1024)(128)(4,1)S(1)}, s32[]{:S(2)}) async-start(s8[8192000]{0:T(1024)(128)(4,1)} %bitcast.168), calls=%async_computation.8 | async-start | bytes 8388608
  105.3 16.8 %slice-start = ((s8[8192000]{0:T(1024)(128)(4,1)}), s8[4194304]{0:T(1024)(128)(4,1)S(1)}, s32[]{:S(2)}) async-start(s8[8192000]{0:T(1024)(128)(4,1)} %bitcast.166), calls=%async_computation.6 | async-start | bytes 8388608
  112.0 4.6 %slice-start.3 = ((s8[8192000]{0:T(1024)(128)(4,1)}), s8[3997696]{0:T(1024)(128)(4,1)S(1)}, s32[]{:S(2)}) async-start(s8[8192000]{0:T(1024)(128)(4,1)} %bitcast.168), calls=%async_computation.9 | async-start | bytes 7995392
  112.0 10.1 %slice-start.1 = ((s8[8192000]{0:T(1024)(128)(4,1)}), s8[3997696]{0:T(1024)(128)(4,1)S(1)}, s32[]{:S(2)}) async-start(s8[8192000]{0:T(1024)(128)(4,1)} %bitcast.166), calls=%async_computation.7 | async-start | bytes 7995392
  116.6 11.0 %slice-start.4 = ((s8[8192000]{0:T(1024)(128)(4,1)}), s8[3997696]{0:T(1024)(128)(4,1)S(1)}, s32[]{:S(2)}) async-start(s8[8192000]{0:T(1024)(128)(4,1)} %bitcast.170), calls=%async_computation.10 | async-start | bytes 7995392
  122.1 5.6 %slice-start.5 = ((s8[8192000]{0:T(1024)(128)(4,1)}), s8[4194304]{0:T(1024)(128)(4,1)S(1)}, s32[]{:S(2)}) async-start(s8[8192000]{0:T(1024)(128)(4,1)} %bitcast.170), calls=%async_computation.11 | async-start | bytes 8388608
  144.1 2.6 copy-start.2
  144.1 39.0 %copy-start.16 = (f32[16,25,36]{2,1,0:T(8,128)S(1)}, f32[16,25,36]{2,1,0:T(8,128)}, u32[]{:S(2)}) copy-start(f32[16,25,36]{2,1,0:T(8,128)} %get-tuple-element.65) | copy-start | bytes 172804
  144.1 39.0 %copy-start.17 = (f32[16,25,36]{2,1,0:T(8,128)S(1)}, f32[16,25,36]{2,1,0:T(8,128)}, u32[]{:S(2)}) copy-start(f32[16,25,36]{2,1,0:T(8,128)} %get-tuple-element.67) | copy-start | bytes 172804
  144.1 39.0 %copy-start.18 = (f32[16,25,36]{2,1,0:T(8,128)S(1)}, f32[16,25,36]{2,1,0:T(8,128)}, u32[]{:S(2)}) copy-start(f32[16,25,36]{2,1,0:T(8,128)} %get-tuple-element.69) | copy-start | bytes 172804
  144.1 39.0 %copy-start.19 = (f32[16,25,36]{2,1,0:T(8,128)S(1)}, f32[16,25,36]{2,1,0:T(8,128)}, u32[]{:S(2)}) copy-start(f32[16,25,36]{2,1,0:T(8,128)} %get-tuple-element.71) | copy-start | bytes 172804
  147.1 8.6 %all-to-all-start.2 = ((f32[8,1,2]{2,1,0:T(1,128)}), f32[8,1,2]{2,1,0:T(1,128)S(1)}, u32[]{:S(2)}, u32[]{:S(2)}) async-start(f32[8,1,2]{2,1,0:T(1,128)} %bitcast.27), calls=%async_computation.2 | async-start | bytes 8192 | tf_op jit(solution)/shard_map/all_to_all | solution.py:242
  155.6 8.5 %all-to-all-start.4 = ((f32[8,1,2]{2,1,0:T(1,128)}), f32[8,1,2]{2,1,0:T(1,128)S(1)}, u32[]{:S(2)}, u32[]{:S(2)}) async-start(f32[8,1,2]{2,1,0:T(1,128)} %bitcast.30), calls=%async_computation.4 | async-start | bytes 8192 | tf_op jit(solution)/shard_map/all_to_all | solution.py:245
  165.3 8.5 %all-to-all-start.5 = ((f32[8,1,2]{2,1,0:T(1,128)}), f32[8,1,2]{2,1,0:T(1,128)S(1)}, u32[]{:S(2)}, u32[]{:S(2)}) async-start(f32[8,1,2]{2,1,0:T(1,128)} %copy.101), calls=%async_computation.5 | async-start | bytes 8192 | tf_op jit(solution)/shard_map/all_to_all | solution.py:257
  173.7 8.6 %all-to-all-start.3 = ((f32[8,1,2]{2,1,0:T(1,128)}), f32[8,1,2]{2,1,0:T(1,128)S(1)}, u32[]{:S(2)}, u32[]{:S(2)}) async-start(f32[8,1,2]{2,1,0:T(1,128)} %copy.98), calls=%async_computation.3 | async-start | bytes 8192 | tf_op jit(solution)/shard_map/all_to_all | solution.py:256
  183.6 1.4 copy-start.7
  188.1 1.4 copy-start.10
  192.5 1.4 copy-start.9
  197.2 1.4 copy-start.5
  271.3 2.4 copy-start.1

commit v2 on v1

v2 whole, which is shorter than its diff:
```python
import math
import numpy as np
import jax, jax.numpy as jnp
from jax import lax
from jax.experimental import pallas as pl
from jax.experimental.pallas import tpu as pltpu
from jax.sharding import PartitionSpec as P

MESH = pl.DeviceIdType.MESH
CYCLES, ANGLES, ROTS, SHIFTS, BOX = 128, 144, 36, 5, 256
CLS_LOC, NCH, RC, LEAD, DROWS = 25, 3, 80, 15, 225
GROUPS, SLOTS, PART = 8, 16, 4
NEGATIVE = -1e30
WIDTH, LHS_ROWS, ACC_ROWS = 1024, 48, 40


def unit_tables():
    angle = 2.0 * math.pi * np.arange(ANGLES) / ANGLES
    radius = np.arange(1, CYCLES + 1)
    out = np.zeros((2, 2, 4, ACC_ROWS, CYCLES), np.float64)
    for axis, along in enumerate((np.cos(angle), np.sin(angle))):
        phase = (2.0 * math.pi / BOX) * along[:, None] * radius
        for part, value in enumerate((np.cos(phase), np.sin(phase))):
            out[axis, part, :, :ROTS] = value.reshape(ROTS, 4, CYCLES).transpose(1, 0, 2)
    return out.astype(np.float32)


def gather_kernel(p_ref, meta_ref, out_ref, mout_ref, lsem, ssem, rsem):
    me = lax.axis_index("cls")
    core = me % 2
    right, left, across = (me + 2) % GROUPS, (me + 6) % GROUPS, (me + 4) % GROUPS
    pair = me + 1 - 2 * core
    shift = pair - me
    barrier = pltpu.get_barrier_semaphore()
    for k in range(1, GROUPS):
        pl.semaphore_signal(barrier, inc=1, device_id={"cls": (me + k) % GROUPS}, device_id_type=MESH)
    pl.semaphore_wait(barrier, GROUPS - 1)
    h0, h1 = pl.ds(0, 2), pl.ds(2, 2)
    sends = []

    def send(src, dst, i, target):
        copy = pltpu.make_async_remote_copy(src_ref=src, dst_ref=dst, send_sem=ssem.at[i], recv_sem=rsem.at[i],
                                            device_id={"cls": target}, device_id_type=MESH)
        copy.start()
        sends.append(copy)
        return copy

    metas = [send(meta_ref, mout_ref.at[me], 13 + k, (me + k) % GROUPS) for k in range(1, GROUPS)]
    r0 = send(p_ref.at[h0], out_ref.at[me, h0], 0, right)
    l1 = send(p_ref.at[h1], out_ref.at[me, h1], 1, left)
    r1 = send(p_ref.at[h1], out_ref.at[me, h1], 2, right)
    l0 = send(p_ref.at[h0], out_ref.at[me, h0], 3, left)
    own = send(p_ref, out_ref.at[me], 4, pair)
    local = pltpu.make_async_copy(p_ref, out_ref.at[me], lsem.at[0])
    local.start()
    mlocal = pltpu.make_async_copy(meta_ref, mout_ref.at[me], lsem.at[1])
    mlocal.start()
    r0.wait_recv()
    fr = send(out_ref.at[left, h0], out_ref.at[left, h0], 5, right)
    s0 = send(out_ref.at[left, h0], out_ref.at[left, h0], 7, pair)
    l1.wait_recv()
    fl = send(out_ref.at[right, h1], out_ref.at[right, h1], 6, left)
    s1 = send(out_ref.at[right, h1], out_ref.at[right, h1], 8, pair)
    r1.wait_recv()
    s2 = send(out_ref.at[left, h1], out_ref.at[left, h1], 9, pair)
    l0.wait_recv()
    s3 = send(out_ref.at[right, h0], out_ref.at[right, h0], 10, pair)
    fr.wait_recv()
    s4 = send(out_ref.at[across, h0], out_ref.at[across, h0], 11, pair)
    fl.wait_recv()
    s5 = send(out_ref.at[across, h1], out_ref.at[across, h1], 12, pair)
    for copy in [own, s0, s1, s2, s3, s4, s5] + metas:
        copy.wait_recv()
    local.wait()
    mlocal.wait()
    for copy in sends:
        copy.wait_send()


def gather_particles(images, meta):
    vmem = pl.BlockSpec(memory_space=pltpu.VMEM)
    return pl.pallas_call(
        gather_kernel,
        out_shape=(jax.ShapeDtypeStruct((GROUPS, PART, 288, 128), jnp.bfloat16),
                   jax.ShapeDtypeStruct((GROUPS, 8, 128), jnp.int32)),
        in_specs=[vmem, vmem],
        out_specs=(vmem, vmem),
        scratch_shapes=[pltpu.SemaphoreType.DMA((2,)), pltpu.SemaphoreType.DMA((21,)), pltpu.SemaphoreType.DMA((21,))],
        compiler_params=pltpu.CompilerParams(collective_id=1, has_side_effects=True, vmem_limit_bytes=16 << 20),
        name="gather_particles",
    )(images, meta)


def group_turn(lane):
    return lane - jnp.where(lane >= 80, 80, jnp.where(lane >= 40, 40, 0))


def lane_places(rows):
    row = lax.broadcasted_iota(jnp.int32, (rows, 128), 0)
    lane = lax.broadcasted_iota(jnp.int32, (rows, 128), 1)
    return row, lane, group_turn(lane)


def score_kernel(meta, unit, images, refs, scores, moved, stats, table, wide, powers):
    slot = pl.program_id(0)
    owner = lax.axis_index("cls")

    @pl.when(slot == 0)
    def _():
        for v in range(GROUPS):
            table[2 * v * 8 + 5] = 0
            table[(2 * v + 1) * 8 + 5] = 0
            place = jnp.int32(2 * v)
            for i in range(PART):
                k = jnp.int32(0)
                for t in range(8):
                    c = meta[v, i, t] - owner * CLS_LOC
                    table[place * 8 + k] = c
                    k = k + jnp.where((c >= 0) & (c < CLS_LOC), 1, 0)
                hit = jnp.where(k > 0, 1, 0)

                @pl.when(hit > 0)
                def _():
                    table[place * 8 + 5] = 1
                    table[place * 8 + 6] = PART * v + i

                place = place + hit
        wide[288:320, :] = jnp.zeros((32, 128), jnp.float32)
        for axis in range(2):
            powers[axis, 0, 0] = jnp.ones((4, ACC_ROWS, 128), jnp.float32)
            powers[axis, 0, 1] = jnp.zeros((4, ACC_ROWS, 128), jnp.float32)
            powers[axis, 1] = unit[axis]
            for t in range(2, 8):
                c0, s0 = powers[axis, t - 1, 0], powers[axis, t - 1, 1]
                c1, s1 = unit[axis, 0], unit[axis, 1]
                powers[axis, t, 0] = c0 * c1 - s0 * s1
                powers[axis, t, 1] = s0 * c1 + c0 * s1
        stats[0] = jnp.full((GROUPS * PART, 128), NEGATIVE, jnp.float32)
        stats[1] = jnp.zeros((GROUPS * PART, 128), jnp.float32)

    @pl.when(table[slot * 8 + 5] > 0)
    def _():
        pid = table[slot * 8 + 6]
        v, i = pid // PART, pid % PART
        tx, ty = meta[v, i, 8], meta[v, i, 9]
        ax, ay = jnp.abs(tx), jnp.abs(ty)
        gx = jnp.where(tx < 0, -1.0, 1.0).astype(jnp.float32)
        gy = jnp.where(ty < 0, -1.0, 1.0).astype(jnp.float32)
        wide[0:288, :] = images[v, i].astype(jnp.float32)
        gap8, gap48 = jnp.zeros((8, 128), jnp.float32), jnp.zeros((48, 128), jnp.float32)
        for a in range(4):
            re = wide[pl.ds(2 * a, ACC_ROWS, stride=8), :]
            im = wide[pl.ds(2 * a + 1, ACC_ROWS, stride=8), :]
            cx, sx = powers[0, ax, 0, a], powers[0, ax, 1, a] * gx
            cy, sy = powers[1, ay, 0, a], powers[1, ay, 1, a] * gy
            bc, bs = cx * cy - sx * sy, sx * cy + cx * sy
            zr, zi = re * bc + im * bs, im * bc - re * bs
            real, imag = [zr], [zi]
            for axis in range(2):
                uc, us = unit[axis, 0, a], unit[axis, 1, a]
                rc, rs, ic, js = zr * uc, zr * us, zi * uc, zi * us
                real += [rc + js, rc - js]
                imag += [ic - rs, ic + rs]
            for m, part in enumerate((real, imag)):
                lanes = pl.ds(256 * a + 128 * m, 128)
                moved[0, 0:128, lanes] = jnp.concatenate(part[0:3] + [gap8], axis=0).astype(jnp.bfloat16)
                moved[0, 128:256, lanes] = jnp.concatenate(part[3:5] + [gap48], axis=0).astype(jnp.bfloat16)
        lhs = jnp.concatenate([refs[table[slot * 8 + k]] for k in range(4)], axis=0)
        pairs = lax.dot_general(lhs, moved[0], (((1,), (1,)), ((), ())), preferred_element_type=jnp.float32)
        row = lax.broadcasted_iota(jnp.int32, (ACC_ROWS, 128), 0)
        lane = lax.broadcasted_iota(jnp.int32, (ACC_ROWS, 128), 1)
        turn = group_turn(jnp.where(lane >= ROTS - 1, lane - (ROTS - 1), lane + 128 - (ROTS - 1)))
        turn2 = group_turn(jnp.where(lane == 127, 0, lane + 1))
        back = (ROTS - 1) - row
        direct = (turn + back < ROTS) & (back >= 0)
        wrapped = (turn2 < ROTS) & (turn2 + back >= ROTS)
        _, lane1, turn1 = lane_places(8)
        lines = []
        for half in range(2):
            rows = []
            for k in range(4):
                block = pairs[LHS_ROWS * k:LHS_ROWS * k + ACC_ROWS, 128 * half:128 * half + 128]
                skew = pltpu.roll(block, 0, 1, stride=1, stride_axis=0)
                near = jnp.sum(jnp.where(direct, skew, 0.0), axis=0, keepdims=True)
                far = jnp.sum(jnp.where(wrapped, skew, 0.0), axis=0, keepdims=True)
                rows.append((near, far))
            near = jnp.concatenate([r[0] for r in rows] + [jnp.zeros((4, 128), jnp.float32)], axis=0)
            far = jnp.concatenate([r[1] for r in rows] + [jnp.zeros((4, 128), jnp.float32)], axis=0)
            whole = 2.0 * (pltpu.roll(near, 128 - (ROTS - 1), 1) + pltpu.roll(far, 1, 1))
            row8 = lax.broadcasted_iota(jnp.int32, (8, 128), 0)
            good = (turn1 < ROTS) & (lane1 < (120 if half == 0 else 80)) & (row8 < 4)
            line = jnp.where(good, whole, NEGATIVE)
            scores[0, :, 128 * half:128 * half + 128] = line
            lines.append(line)
        best = jnp.max(jnp.max(jnp.maximum(lines[0], lines[1]), axis=1, keepdims=True), axis=0, keepdims=True)
        power = jnp.exp(lines[0] - best) + jnp.exp(lines[1] - best)
        mass = jnp.sum(jnp.sum(power, axis=1, keepdims=True), axis=0, keepdims=True)
        stats[0, pl.ds(pid, 1), :] = jnp.broadcast_to(best, (1, 128))
        stats[1, pl.ds(pid, 1), :] = jnp.broadcast_to(mass, (1, 128))


def score_slots(meta, unit, images, refs):
    vmem, smem = pl.BlockSpec(memory_space=pltpu.VMEM), pl.BlockSpec(memory_space=pltpu.SMEM)
    return pl.pallas_call(
        score_kernel,
        grid=(SLOTS,),
        out_shape=(jax.ShapeDtypeStruct((SLOTS, 8, 256), jnp.float32),
                   jax.ShapeDtypeStruct((SLOTS, 256, WIDTH), jnp.bfloat16),
                   jax.ShapeDtypeStruct((2, GROUPS * PART, 128), jnp.float32),
                   jax.ShapeDtypeStruct((17 * 8,), jnp.int32)),
        in_specs=[smem, vmem, vmem, vmem],
        out_specs=(pl.BlockSpec((1, 8, 256), lambda i: (i, 0, 0)),
                   pl.BlockSpec((1, 256, WIDTH), lambda i: (i, 0, 0)), vmem, smem),
        scratch_shapes=[pltpu.VMEM((320, 128), jnp.float32),
                        pltpu.VMEM((2, 8, 2, 4, ACC_ROWS, 128), jnp.float32)],
        compiler_params=pltpu.CompilerParams(vmem_limit_bytes=40 << 20),
        name="score_slots",
    )(meta, unit, images, refs)


def norm_kernel(stats, total, boxes, ssem, rsem):
    me = lax.axis_index("cls")
    barrier = pltpu.get_barrier_semaphore()
    for k in range(1, GROUPS):
        pl.semaphore_signal(barrier, inc=1, device_id={"cls": (me + k) % GROUPS}, device_id_type=MESH)
    pl.semaphore_wait(barrier, GROUPS - 1)
    copies = []
    for k in range(1, GROUPS):
        copy = pltpu.make_async_remote_copy(src_ref=stats, dst_ref=boxes.at[k - 1], send_sem=ssem.at[k - 1],
                                            recv_sem=rsem.at[k - 1], device_id={"cls": (me + k) % GROUPS},
                                            device_id_type=MESH)
        copy.start()
        copies.append(copy)
    for copy in copies:
        copy.wait_recv()
    best = stats[0]
    for k in range(GROUPS - 1):
        best = jnp.maximum(best, boxes[k, 0])
    whole = stats[1] * jnp.exp(stats[0] - best)
    for k in range(GROUPS - 1):
        whole = whole + boxes[k, 1] * jnp.exp(boxes[k, 0] - best)
    total[0] = best
    total[1] = whole
    for copy in copies:
        copy.wait_send()


def normalise(stats):
    vmem = pl.BlockSpec(memory_space=pltpu.VMEM)
    return pl.pallas_call(
        norm_kernel,
        out_shape=jax.ShapeDtypeStruct((2, GROUPS * PART, 128), jnp.float32),
        in_specs=[vmem],
        out_specs=vmem,
        scratch_shapes=[pltpu.VMEM((GROUPS - 1, 2, GROUPS * PART, 128), jnp.float32),
                        pltpu.SemaphoreType.DMA((7,)), pltpu.SemaphoreType.DMA((7,))],
        compiler_params=pltpu.CompilerParams(collective_id=2, has_side_effects=True),
        name="normalise",
    )(stats)


def sum_kernel(table, total, scores, moved, out, acc, comp, masses):
    slot = pl.program_id(0)

    @pl.when(slot == 0)
    def _():
        acc[...] = jnp.zeros(acc.shape, jnp.float32)
        masses[...] = jnp.zeros(masses.shape, jnp.float32)

    @pl.when(table[slot * 8 + 5] > 0)
    def _():
        pid = table[slot * 8 + 6]
        best, whole = total[0, pl.ds(pid, 1), :], total[1, pl.ds(pid, 1), :]
        row, _, turn = lane_places(ACC_ROWS)
        later = turn >= row
        halves = []
        mass = jnp.zeros((8, 1), jnp.float32)
        for half in range(2):
            weight = jnp.exp(scores[0, :, 128 * half:128 * half + 128] - best) / whole
            weight = weight.astype(jnp.bfloat16).astype(jnp.float32)
            mass = mass + jnp.sum(weight, axis=1, keepdims=True)
            back = pltpu.roll(weight, 92, 1)
            rows = []
            for k in range(4):
                one = jnp.broadcast_to(weight[k:k + 1, :], (ACC_ROWS, 128))
                two = jnp.broadcast_to(back[k:k + 1, :], (ACC_ROWS, 128))
                rows.append(jnp.where(later, pltpu.roll(one, 0, 1, stride=1, stride_axis=0),
                                      pltpu.roll(two, 0, 1, stride=1, stride_axis=0)))
            halves.append(jnp.concatenate(rows, axis=0))
        spread = jnp.concatenate(halves, axis=1).astype(jnp.bfloat16)
        for k in range(4):
            c = table[slot * 8 + k]
            masses[pl.ds(c, 1), :] = masses[pl.ds(c, 1), :] + jnp.broadcast_to(mass[k:k + 1, :], (1, 128))
        contrib = jnp.dot(spread, moved[0], preferred_element_type=jnp.float32)
        for k in range(4):
            c = table[slot * 8 + k]
            acc[c] = acc[c] + contrib[ACC_ROWS * k:ACC_ROWS * (k + 1)]

    @pl.when(slot == SLOTS - 1)
    def _():
        row = lax.broadcasted_iota(jnp.int32, (32, 128), 0)
        lane = lax.broadcasted_iota(jnp.int32, (32, 128), 1)
        line = jnp.sum(jnp.where(row == lane, masses[...], 0.0), axis=0, keepdims=True)
        high = line.astype(jnp.bfloat16).astype(jnp.float32)
        lead = jnp.concatenate([high, line - high, jnp.zeros((14, 128), jnp.float32)], axis=0)
        for y in range(4):
            comp[y * 240:y * 240 + 16, :] = jnp.concatenate([lead] * 8, axis=1)
        for c in range(CLS_LOC):
            start = c * ROTS
            while start < (c + 1) * ROTS:
                y = start // DROWS
                stop = min((c + 1) * ROTS, (y + 1) * DROWS)
                to = y * 240 + LEAD + start - y * DROWS
                comp[to:to + stop - start, :] = acc[c, start - c * ROTS:stop - c * ROTS, :]
                start = stop
        for ch in range(NCH):
            for y in range(4):
                for z in range(8):
                    out[ch, y, z] = comp[y * 240 + ch * RC:y * 240 + (ch + 1) * RC,
                                         128 * z:128 * z + 128].astype(jnp.bfloat16)


def sum_slots(table, total, scores, moved):
    vmem, smem = pl.BlockSpec(memory_space=pltpu.VMEM), pl.BlockSpec(memory_space=pltpu.SMEM)
    return pl.pallas_call(
        sum_kernel,
        grid=(SLOTS,),
        out_shape=jax.ShapeDtypeStruct((NCH, 4, 8, RC, 128), jnp.bfloat16),
        in_specs=[smem, vmem, pl.BlockSpec((1, 8, 256), lambda i: (i, 0, 0)),
                  pl.BlockSpec((1, 256, WIDTH), lambda i: (i, 0, 0))],
        out_specs=vmem,
        scratch_shapes=[pltpu.VMEM((CLS_LOC, ACC_ROWS, WIDTH), jnp.float32),
                        pltpu.VMEM((960, WIDTH), jnp.float32),
                        pltpu.VMEM((32, 128), jnp.float32)],
        compiler_params=pltpu.CompilerParams(vmem_limit_bytes=40 << 20),
        name="sum_slots",
    )(table, total, scores, moved)


def reduce_kernel(p_ref, g_ref, x1, x2, d3, d4, e5, e6, c1, c2, s_buf, z_buf, ysend, yrecv, zsend, zrecv):
    dom = lax.axis_index("dom")
    y = dom % 4
    z = dom // 4
    yp, ym, yo = (y + 1) % 4, (y + 3) % 4, (y + 2) % 4
    up, down = {"dom": z * 4 + yp}, {"dom": z * 4 + ym}
    zdev = [{"dom": ((z + k) % 8) * 4 + y} for k in range(8)]
    barrier = pltpu.get_barrier_semaphore()
    for target in [up, down] + zdev[1:]:
        pl.semaphore_signal(barrier, inc=1, device_id=target, device_id_type=MESH)
    pl.semaphore_wait(barrier, 9)
    A, B = pl.ds(0, 4), pl.ds(4, 4)

    def send(src, dst, ssem, rsem, target):
        copy = pltpu.make_async_remote_copy(src_ref=src, dst_ref=dst, send_sem=ssem, recv_sem=rsem,
                                            device_id=target, device_id_type=MESH)
        copy.start()
        return copy

    pending = []
    m1, m2, m3, m4, m5, m6 = {}, {}, {}, {}, {}, {}
    for ch in range(NCH):
        m1[ch] = send(p_ref.at[ch, yo, A], x1.at[ch], ysend.at[ch, 0], yrecv.at[ch, 0], up)
        m2[ch] = send(p_ref.at[ch, yo, B], x2.at[ch], ysend.at[ch, 1], yrecv.at[ch, 1], down)
        m3[ch] = send(p_ref.at[ch, yp, B], d3.at[ch], ysend.at[ch, 2], yrecv.at[ch, 2], up)
        m4[ch] = send(p_ref.at[ch, ym, A], d4.at[ch], ysend.at[ch, 3], yrecv.at[ch, 3], down)
    for ch in range(NCH):
        m1[ch].wait_recv()
        c1[ch] = (x1[ch].astype(jnp.float32) + p_ref[ch, yp, A].astype(jnp.float32)).astype(jnp.bfloat16)
        m5[ch] = send(c1.at[ch], e5.at[ch], ysend.at[ch, 4], yrecv.at[ch, 4], up)
        m2[ch].wait_recv()
        c2[ch] = (x2[ch].astype(jnp.float32) + p_ref[ch, ym, B].astype(jnp.float32)).astype(jnp.bfloat16)
        m6[ch] = send(c2.at[ch], e6.at[ch], ysend.at[ch, 5], yrecv.at[ch, 5], down)
    zm = {}
    for ch in range(NCH):
        m4[ch].wait_recv()
        m5[ch].wait_recv()
        s_buf[ch, A] = (p_ref[ch, y, A].astype(jnp.float32) + e5[ch].astype(jnp.float32)
                        + d4[ch].astype(jnp.float32)).astype(jnp.bfloat16)
        m3[ch].wait_recv()
        m6[ch].wait_recv()
        s_buf[ch, B] = (p_ref[ch, y, B].astype(jnp.float32) + e6[ch].astype(jnp.float32)
                        + d3[ch].astype(jnp.float32)).astype(jnp.bfloat16)
        for k in range(1, 8):
            zm[ch, k] = send(s_buf.at[ch, (z + k) % 8], z_buf.at[ch, k - 1],
                             zsend.at[ch, k - 1], zrecv.at[ch, k - 1], zdev[k])
    zg = {}
    mass = None
    for ch in range(NCH):
        num = s_buf[ch, z].astype(jnp.float32)
        for k in range(1, 8):
            zm[ch, k].wait_recv()
            num = num + z_buf[ch, k - 1].astype(jnp.float32)
        if ch == 0:
            mass = num[0:1, :] + num[1:2, :] + 1.0
        place = DROWS * y + (ch * RC - LEAD) + lax.broadcasted_iota(jnp.int32, (RC, 128), 0)
        den = jnp.ones((RC, 128), jnp.float32)
        for c in range(CLS_LOC):
            here = (place >= c * ROTS) & (place < (c + 1) * ROTS)
            den = jnp.where(here, jnp.broadcast_to(mass[:, c:c + 1], (RC, 128)), den)
        g_ref[ch, y, z] = (num / den).astype(jnp.bfloat16)
        for k in range(1, 8):
            zg[ch, k] = send(g_ref.at[ch, y, z], g_ref.at[ch, y, z],
                             zsend.at[ch, 6 + k], zrecv.at[ch, 6 + k], zdev[k])
    m7, m8, m9, m10 = {}, {}, {}, {}
    for ch in range(NCH):
        for k in range(1, 8):
            zg[ch, k].wait_recv()
        m7[ch] = send(g_ref.at[ch, y], g_ref.at[ch, y], ysend.at[ch, 6], yrecv.at[ch, 6], up)
        m8[ch] = send(g_ref.at[ch, y], g_ref.at[ch, y], ysend.at[ch, 7], yrecv.at[ch, 7], down)
    for ch in range(NCH):
        m7[ch].wait_recv()
        m9[ch] = send(g_ref.at[ch, ym, A], g_ref.at[ch, ym, A], ysend.at[ch, 8], yrecv.at[ch, 8], up)
        m8[ch].wait_recv()
        m10[ch] = send(g_ref.at[ch, yp, B], g_ref.at[ch, yp, B], ysend.at[ch, 9], yrecv.at[ch, 9], down)
    for ch in range(NCH):
        m9[ch].wait_recv()
        m10[ch].wait_recv()
    for group in (m1, m2, m3, m4, m5, m6, zm, zg, m7, m8, m9, m10):
        for copy in group.values():
            copy.wait_send()


def reduce_average(payload):
    half = pltpu.VMEM((NCH, 4, RC, 128), jnp.bfloat16)
    return pl.pallas_call(
        reduce_kernel,
        out_shape=jax.ShapeDtypeStruct((NCH, 4, 8, RC, 128), jnp.bfloat16),
        in_specs=[pl.BlockSpec(memory_space=pltpu.VMEM)],
        out_specs=pl.BlockSpec(memory_space=pltpu.VMEM),
        scratch_shapes=[half] * 8 + [
            pltpu.VMEM((NCH, 8, RC, 128), jnp.bfloat16),
            pltpu.VMEM((NCH, 7, RC, 128), jnp.bfloat16),
            pltpu.SemaphoreType.DMA((NCH, 10)),
            pltpu.SemaphoreType.DMA((NCH, 10)),
            pltpu.SemaphoreType.DMA((NCH, 14)),
            pltpu.SemaphoreType.DMA((NCH, 14)),
        ],
        compiler_params=pltpu.CompilerParams(collective_id=5, has_side_effects=True, vmem_limit_bytes=40 << 20),
        name="reduce_average",
    )(payload)


def unpack_average(gathered):
    rows = gathered.transpose(1, 0, 3, 2, 4).reshape(4, NCH * RC, 8, 128)[:, LEAD:]
    return rows.reshape(CLS_LOC, 36864)


def shards(particles, references, candidates, offsets):
    meta = jnp.pad(jnp.concatenate([candidates, offsets], axis=1), ((0, 4), (0, 118)))
    images, meta = gather_particles(particles.reshape(PART, 288, 128), meta)
    refs = jnp.pad(references.reshape(CLS_LOC, ROTS, WIDTH)[:, ::-1], ((0, 0), (0, LHS_ROWS - ROTS), (0, 0)))
    scores, moved, stats, table = score_slots(meta, jnp.asarray(unit_tables()), images, refs)
    payload = sum_slots(table, normalise(stats), scores, moved)
    return unpack_average(reduce_average(payload))


def solution(mesh):
    in_specs = (
        P(("cls", "dom"), None),
        P("cls", None),
        P(("cls", "dom"), None),
        P(("cls", "dom"), None),
    )
    return jax.shard_map(shards, mesh=mesh, in_specs=in_specs, out_specs=P("cls", None), check_vma=False)
```

time: 277 us -> 126 us (0.45)
  matrix products: 88.8 us -> 0 us
  Pallas kernels: 58.1 us -> 101 us
  other arithmetic: 38.9 us -> 0.75 us
  waiting for transfers between devices: 32.4 us -> 0 us
  starting transfers between devices: 21.8 us -> 0 us
  local copies, waits for them, and re-layouts: 33.1 us -> 22.2 us
    dot_general x22 -> x0, matrix products: 88.8 us -> none  [the longest x5 36.1 us: shards(): jnp.einsum('xjf,clf->xjcl', moved, class_refs, preferred_element_type=jnp...]
    pallas_call x0 -> x4, Pallas kernels: none -> 42.5 us  [the longest x1 16.8 us: gather_particles(): pl.pallas_call(gather_kernel, out_shape=(jax.ShapeDtypeStruct((GROUPS, PA...]
    all_to_all x6 -> x0, waiting for transfers between devices: 32.4 us -> none  [the longest x1 12.4 us: shards(): lax.all_to_all(outgoing, 'cls', split_axis=0, concat_axis=0, tiled=True)]
    add x4 -> x0, other arithmetic: 28.6 us -> none  [the longest x2 28.6 us: shift_images(): real_part * cosine + imag_part * sine]
    all_to_all x6 -> x0, starting transfers between devices: 21.8 us -> none  [the longest x1 4.3 us: shards(): lax.all_to_all(meta_out, 'cls', split_axis=0, concat_axis=0, tiled=True)]
    convert_element_type x13 -> x0, local copies, waits for them, and re-layouts: 16.9 us -> none  [the longest x10 13.7 us: shift_images(): return jnp.stack([real_part * cosine + imag_part * sine, imag_part * cosi...]
    unnamed x53 -> x12, local copies, waits for them, and re-layouts: 0.88 us -> 9.73 us
    rev x0 -> x1, local copies, waits for them, and re-layouts: none -> 5.13 us  [shards(): references.reshape(CLS_LOC, ROTS, WIDTH)[:, ::-1]]
  transfers between devices with their start and end apart: 6 -> 0, of which waited for: 6 -> 0; matrix products, arithmetic and copies ran while one was open for 4% -> 0% of each run, Pallas kernels for 0% -> 0%
where the time goes in v2:
time: 126 us; the launch traced here: 124 us
  Pallas kernels  101 us (80%)
  local copies, waits for them, and re-layouts  22.2 us (18%)
    pallas_call x1, Pallas kernels, reduce_average(): pl.pallas_call(reduce_kernel, out_shape=jax.ShapeDtypeStruct((NCH, 4, 8,...  58.3 us
    pallas_call x1, Pallas kernels, gather_particles(): pl.pallas_call(gather_kernel, out_shape=(jax.ShapeDtypeStruct((GROUPS, PA...  16.8 us
    pallas_call x1, Pallas kernels, score_slots(): pl.pallas_call(score_kernel, grid=(SLOTS,), out_shape=(jax.ShapeDtypeStru...  10.7 us
    unnamed x12, local copies, waits for them, and re-layouts  9.73 us
    pallas_call x1, Pallas kernels, normalise(): pl.pallas_call(norm_kernel, out_shape=jax.ShapeDtypeStruct((2, GROUPS * P...  9.17 us
    pallas_call x1, Pallas kernels, sum_slots(): pl.pallas_call(sum_kernel, grid=(SLOTS,), out_shape=jax.ShapeDtypeStruct(...  5.78 us
    rev x1, local copies, waits for them, and re-layouts, shards(): references.reshape(CLS_LOC, ROTS, WIDTH)[:, ::-1]  5.13 us
    reshape x1, local copies, waits for them, and re-layouts, shards(): references.reshape(CLS_LOC, ROTS, WIDTH)[:, ::-1]  4.09 us

profile of v2, /device:TPU:8, one launch (start us, length us, event | category | flops | bytes accessed | tf_op | source)
XLA Modules:
  0.0 123.7 jit_solution(13821386378689163849)
XLA Ops:
  0.0 0.8 copy.7
  0.8 0.8 pad_add_fusion
  1.5 1.0 copy.11
  2.5 4.1 %reshape.13 = bf16[25,36,1024]{2,1,0:T(8,128)(2,1)} reshape(bf16[25,36864]{1,0:T(8,128)(2,1)} %param.6) | data formatting | bytes 3686400 | tf_op jit(solution)/shard_map/reshape | solution.py:451
  6.6 5.1 %rev.3 = bf16[25,36,1024]{2,1,0:T(8,128)(2,1)S(1)} reverse(bf16[25,36,1024]{2,1,0:T(8,128)(2,1)} %reshape.13), dimensions={1} | reverse | bytes 3686400 | tf_op jit(solution)/shard_map/rev | solution.py:451
  11.8 0.0 copy-start.2
  11.8 0.3 pad.9.refs
  12.1 16.8 %gather_particles.1 = (bf16[8,4,288,128]{3,2,1,0:T(8,128)(2,1)S(1)}, s32[8,8,128]{2,1,0:T(8,128)S(1)}) custom-call(bf16[4,288,128]{2,1,0:T(8,128)(2,1)S(1)} %bitcast.9, s32[8,128]{1,0:T(8,128)S(1)} %pad.8.meta_ref), custom_call_target="tpu_custom_call" | custom-call | tf_op jit(solution)/shard_map/gather_particles/pallas_call | solution.py:82
  28.9 0.0 copy-done.2
  28.9 10.7 %score_slots.1 = (f32[16,8,256]{2,1,0:T(8,128)S(1)}, bf16[16,256,1024]{2,1,0:T(8,128)(2,1)S(1)}, f32[2,32,128]{2,1,0:T(8,128)S(1)}, s32[136]{0:T(256)S(1)}) custom-call(s32[8,8,128]{2,1,0:T(8,128)S(1)} %get-tuple-element.11.meta, f32[2,2,4,40,128]{4,3,2,1,0:T(8,128)S(1)} %copy-done.2, bf16[8,4,288,128]{3,2,1,0:T(8,128)(2,1)S(1)} %get-tuple-element.12.images, ...), custom_call_target="tpu_custom_call" | custom-call | tf_op jit(solution)/shard_map/score_slots/pallas_call | solution.py:204
  39.6 0.0 copy-start
  39.7 3.2 %copy-done = bf16[16,256,1024]{2,1,0:T(8,128)(2,1)} copy-done((bf16[16,256,1024]{2,1,0:T(8,128)(2,1)}, bf16[16,256,1024]{2,1,0:T(8,128)(2,1)S(1)}, u32[]{:S(2)}) %copy-start) | copy-done | bytes 8388632
  42.9 0.0 copy-start.4
  42.9 0.6 copy-done.4
  43.5 9.2 %normalise.1.total = f32[2,32,128]{2,1,0:T(8,128)} custom-call(f32[2,32,128]{2,1,0:T(8,128)} %copy-done.4), custom_call_target="tpu_custom_call" | custom-call | tf_op jit(solution)/shard_map/normalise/pallas_call | solution.py:250
  52.7 0.0 copy-start.1
  52.7 3.4 %copy-done.1 = bf16[16,256,1024]{2,1,0:T(8,128)(2,1)S(1)} copy-done((bf16[16,256,1024]{2,1,0:T(8,128)(2,1)S(1)}, bf16[16,256,1024]{2,1,0:T(8,128)(2,1)}, u32[]{:S(2)}) %copy-start.1) | copy-done | bytes 8388632
  56.0 0.0 copy-start.3
  56.0 0.8 copy-done.3
  56.8 5.8 %sum_slots.1.p_ref = bf16[3,4,8,80,128]{4,3,2,1,0:T(8,128)(2,1)S(1)} custom-call(s32[136]{0:T(256)S(1)} %get-tuple-element.13.table, f32[2,32,128]{2,1,0:T(8,128)S(1)} %copy-done.3, f32[16,8,256]{2,1,0:T(8,128)S(1)} %get-tuple-element.15.scores, bf16[16,256,1024]{2,1,0:T(8,128)(2,1)S(1)} %copy-done.1), custom_call_target="tpu_custom_call" | custom-call | tf_op jit(solution)/shard_map/sum_slots/pallas_call | solution.py:325
  62.6 58.3 %reduce_average.1 = bf16[3,4,8,80,128]{4,3,2,1,0:T(8,128)(2,1)S(1)} custom-call(bf16[3,4,8,80,128]{4,3,2,1,0:T(8,128)(2,1)S(1)} %sum_slots.1.p_ref), custom_call_target="tpu_custom_call" | custom-call | tf_op jit(solution)/shard_map/reduce_average/pallas_call | solution.py:425
  120.9 0.5 copy.8
  121.4 0.1 slice.4
  121.5 2.2 %reshape.15 = bf16[25,36864]{1,0:T(8,128)(2,1)} reshape(bf16[4,225,8,128]{3,2,1,0:T(8,128)(2,1)S(1)} %slice.4) | data formatting | bytes 3686400 | tf_op jit(solution)/shard_map/reshape | solution.py:445
  (1 shorter events, 0.0 us)
Async XLA Ops:
  11.8 17.1 %copy-start.2 = (f32[2,2,4,40,128]{4,3,2,1,0:T(8,128)S(1)}, f32[2,2,4,40,128]{4,3,2,1,0:T(8,128)}, u32[]{:S(2)}) copy-start(f32[2,2,4,40,128]{4,3,2,1,0:T(8,128)} %constant.6.clone.unit) | copy-start | bytes 983044
  39.6 3.2 %copy-start = (bf16[16,256,1024]{2,1,0:T(8,128)(2,1)}, bf16[16,256,1024]{2,1,0:T(8,128)(2,1)S(1)}, u32[]{:S(2)}) copy-start(bf16[16,256,1024]{2,1,0:T(8,128)(2,1)S(1)} %get-tuple-element.16.moved) | copy-start | bytes 25165828
  42.9 0.6 copy-start.4
  52.7 3.4 %copy-start.1 = (bf16[16,256,1024]{2,1,0:T(8,128)(2,1)S(1)}, bf16[16,256,1024]{2,1,0:T(8,128)(2,1)}, u32[]{:S(2)}) copy-start(bf16[16,256,1024]{2,1,0:T(8,128)(2,1)} %copy-done) | copy-start | bytes 25165828
  56.0 0.8 copy-start.3

commit v3 on v2

--- a/solution.py
+++ b/solution.py
@@ -8,7 +8,7 @@
 
 MESH = pl.DeviceIdType.MESH
 CYCLES, ANGLES, ROTS, SHIFTS, BOX = 128, 144, 36, 5, 256
-CLS_LOC, NCH, RC, LEAD, DROWS = 25, 3, 80, 15, 225
+CLS_LOC, NCH, RC, LEAD, DROWS = 25, 5, 48, 15, 225
 GROUPS, SLOTS, PART = 8, 16, 4
 NEGATIVE = -1e30
 WIDTH, LHS_ROWS, ACC_ROWS = 1024, 48, 40
@@ -25,7 +25,7 @@
     return out.astype(np.float32)
 
 
-def gather_kernel(p_ref, meta_ref, out_ref, mout_ref, lsem, ssem, rsem):
+def gather_kernel(p_ref, cand_ref, offs_ref, refs_ref, out_ref, cout_ref, oout_ref, rows_ref, tall, lsem, ssem, rsem):
     me = lax.axis_index("cls")
     core = me % 2
     right, left, across = (me + 2) % GROUPS, (me + 6) % GROUPS, (me + 4) % GROUPS
@@ -45,22 +45,45 @@
         sends.append(copy)
         return copy
 
-    metas = [send(meta_ref, mout_ref.at[me], 13 + k, (me + k) % GROUPS) for k in range(1, GROUPS)]
+    metas = [send(cand_ref, cout_ref.at[me], 12 + k, (me + k) % GROUPS) for k in range(1, GROUPS)]
+    metas += [send(offs_ref, oout_ref.at[me], 19 + k, (me + k) % GROUPS) for k in range(1, GROUPS)]
     r0 = send(p_ref.at[h0], out_ref.at[me, h0], 0, right)
     l1 = send(p_ref.at[h1], out_ref.at[me, h1], 1, left)
     r1 = send(p_ref.at[h1], out_ref.at[me, h1], 2, right)
     l0 = send(p_ref.at[h0], out_ref.at[me, h0], 3, left)
     own = send(p_ref, out_ref.at[me], 4, pair)
-    local = pltpu.make_async_copy(p_ref, out_ref.at[me], lsem.at[0])
-    local.start()
-    mlocal = pltpu.make_async_copy(meta_ref, mout_ref.at[me], lsem.at[1])
-    mlocal.start()
+    locals_ = [pltpu.make_async_copy(p_ref, out_ref.at[me], lsem.at[0]),
+               pltpu.make_async_copy(cand_ref, cout_ref.at[me], lsem.at[1]),
+               pltpu.make_async_copy(offs_ref, oout_ref.at[me], lsem.at[2])]
+    for copy in locals_:
+        copy.start()
+
+    def clear(c, carry):
+        for g in range(8):
+            tall[g, pl.ds(pl.multiple_of(c * LHS_ROWS + 32, 16), 16), :] = jnp.zeros((16, 128), jnp.float32)
+        return carry
+
+    def spread(l, carry):
+        value = refs_ref[:, pl.ds(pl.multiple_of(l * WIDTH, WIDTH), WIDTH)].astype(jnp.float32)
+        for g in range(8):
+            tall[g, pl.ds(ROTS - 1 - l, CLS_LOC, stride=LHS_ROWS), :] = value[:, 128 * g:128 * g + 128]
+        return carry
+
+    def pack(c, carry):
+        rows = pl.ds(pl.multiple_of(c * LHS_ROWS, LHS_ROWS), LHS_ROWS)
+        for g in range(8):
+            rows_ref[c, :, 128 * g:128 * g + 128] = tall[g, rows, :].astype(jnp.bfloat16)
+        return carry
+
+    lax.fori_loop(0, CLS_LOC, clear, 0)
+    lax.fori_loop(0, ROTS, spread, 0)
     r0.wait_recv()
     fr = send(out_ref.at[left, h0], out_ref.at[left, h0], 5, right)
     s0 = send(out_ref.at[left, h0], out_ref.at[left, h0], 7, pair)
     l1.wait_recv()
     fl = send(out_ref.at[right, h1], out_ref.at[right, h1], 6, left)
     s1 = send(out_ref.at[right, h1], out_ref.at[right, h1], 8, pair)
+    lax.fori_loop(0, CLS_LOC, pack, 0)
     r1.wait_recv()
     s2 = send(out_ref.at[left, h1], out_ref.at[left, h1], 9, pair)
     l0.wait_recv()
@@ -71,24 +94,27 @@
     s5 = send(out_ref.at[across, h1], out_ref.at[across, h1], 12, pair)
     for copy in [own, s0, s1, s2, s3, s4, s5] + metas:
         copy.wait_recv()
-    local.wait()
-    mlocal.wait()
+    for copy in locals_:
+        copy.wait()
     for copy in sends:
         copy.wait_send()
 
 
-def gather_particles(images, meta):
+def gather_particles(images, candidates, offsets, refs):
     vmem = pl.BlockSpec(memory_space=pltpu.VMEM)
     return pl.pallas_call(
         gather_kernel,
         out_shape=(jax.ShapeDtypeStruct((GROUPS, PART, 288, 128), jnp.bfloat16),
-                   jax.ShapeDtypeStruct((GROUPS, 8, 128), jnp.int32)),
-        in_specs=[vmem, vmem],
-        out_specs=(vmem, vmem),
-        scratch_shapes=[pltpu.SemaphoreType.DMA((2,)), pltpu.SemaphoreType.DMA((21,)), pltpu.SemaphoreType.DMA((21,))],
-        compiler_params=pltpu.CompilerParams(collective_id=1, has_side_effects=True, vmem_limit_bytes=16 << 20),
+                   jax.ShapeDtypeStruct((GROUPS, PART, 8), jnp.int32),
+                   jax.ShapeDtypeStruct((GROUPS, PART, 2), jnp.int32),
+                   jax.ShapeDtypeStruct((CLS_LOC, LHS_ROWS, WIDTH), jnp.bfloat16)),
+        in_specs=[vmem] * 4,
+        out_specs=(vmem,) * 4,
+        scratch_shapes=[pltpu.VMEM((8, CLS_LOC * LHS_ROWS, 128), jnp.float32), pltpu.SemaphoreType.DMA((3,)),
+                        pltpu.SemaphoreType.DMA((27,)), pltpu.SemaphoreType.DMA((27,))],
+        compiler_params=pltpu.CompilerParams(collective_id=1, has_side_effects=True, vmem_limit_bytes=24 << 20),
         name="gather_particles",
-    )(images, meta)
+    )(images, candidates, offsets, refs)
 
 
 def group_turn(lane):
@@ -101,7 +127,7 @@
     return row, lane, group_turn(lane)
 
 
-def score_kernel(meta, unit, images, refs, scores, moved, stats, table, wide, powers):
+def score_kernel(cands, priors, unit, images, refs, scores, moved, stats, table, wide, powers):
     slot = pl.program_id(0)
     owner = lax.axis_index("cls")
 
@@ -114,7 +140,7 @@
             for i in range(PART):
                 k = jnp.int32(0)
                 for t in range(8):
-                    c = meta[v, i, t] - owner * CLS_LOC
+                    c = cands[v, i, t] - owner * CLS_LOC
                     table[place * 8 + k] = c
                     k = k + jnp.where((c >= 0) & (c < CLS_LOC), 1, 0)
                 hit = jnp.where(k > 0, 1, 0)
@@ -135,14 +161,14 @@
                 c1, s1 = unit[axis, 0], unit[axis, 1]
                 powers[axis, t, 0] = c0 * c1 - s0 * s1
                 powers[axis, t, 1] = s0 * c1 + c0 * s1
-        stats[0] = jnp.full((GROUPS * PART, 128), NEGATIVE, jnp.float32)
-        stats[1] = jnp.zeros((GROUPS * PART, 128), jnp.float32)
+        first = lax.broadcasted_iota(jnp.int32, (8, 128), 0) == 0
+        stats[...] = jnp.where(first, NEGATIVE, 0.0)
 
     @pl.when(table[slot * 8 + 5] > 0)
     def _():
         pid = table[slot * 8 + 6]
         v, i = pid // PART, pid % PART
-        tx, ty = meta[v, i, 8], meta[v, i, 9]
+        tx, ty = priors[v, i, 0], priors[v, i, 1]
         ax, ay = jnp.abs(tx), jnp.abs(ty)
         gx = jnp.where(tx < 0, -1.0, 1.0).astype(jnp.float32)
         gy = jnp.where(ty < 0, -1.0, 1.0).astype(jnp.float32)
@@ -195,27 +221,28 @@
         best = jnp.max(jnp.max(jnp.maximum(lines[0], lines[1]), axis=1, keepdims=True), axis=0, keepdims=True)
         power = jnp.exp(lines[0] - best) + jnp.exp(lines[1] - best)
         mass = jnp.sum(jnp.sum(power, axis=1, keepdims=True), axis=0, keepdims=True)
-        stats[0, pl.ds(pid, 1), :] = jnp.broadcast_to(best, (1, 128))
-        stats[1, pl.ds(pid, 1), :] = jnp.broadcast_to(mass, (1, 128))
-
-
-def score_slots(meta, unit, images, refs):
+        place = lax.broadcasted_iota(jnp.int32, (1, 128), 1) == pid
+        stats[0:1, :] = jnp.where(place, best, stats[0:1, :])
+        stats[1:2, :] = jnp.where(place, mass, stats[1:2, :])
+
+
+def score_slots(cands, priors, unit, images, refs):
     vmem, smem = pl.BlockSpec(memory_space=pltpu.VMEM), pl.BlockSpec(memory_space=pltpu.SMEM)
     return pl.pallas_call(
         score_kernel,
         grid=(SLOTS,),
         out_shape=(jax.ShapeDtypeStruct((SLOTS, 8, 256), jnp.float32),
                    jax.ShapeDtypeStruct((SLOTS, 256, WIDTH), jnp.bfloat16),
-                   jax.ShapeDtypeStruct((2, GROUPS * PART, 128), jnp.float32),
+                   jax.ShapeDtypeStruct((8, 128), jnp.float32),
                    jax.ShapeDtypeStruct((17 * 8,), jnp.int32)),
-        in_specs=[smem, vmem, vmem, vmem],
+        in_specs=[smem, smem, vmem, vmem, vmem],
         out_specs=(pl.BlockSpec((1, 8, 256), lambda i: (i, 0, 0)),
                    pl.BlockSpec((1, 256, WIDTH), lambda i: (i, 0, 0)), vmem, smem),
         scratch_shapes=[pltpu.VMEM((320, 128), jnp.float32),
                         pltpu.VMEM((2, 8, 2, 4, ACC_ROWS, 128), jnp.float32)],
-        compiler_params=pltpu.CompilerParams(vmem_limit_bytes=40 << 20),
+        compiler_params=pltpu.CompilerParams(vmem_limit_bytes=28 << 20),
         name="score_slots",
-    )(meta, unit, images, refs)
+    )(cands, priors, unit, images, refs)
 
 
 def norm_kernel(stats, total, boxes, ssem, rsem):
@@ -233,14 +260,13 @@
         copies.append(copy)
     for copy in copies:
         copy.wait_recv()
-    best = stats[0]
+    best = stats[0:1, :]
     for k in range(GROUPS - 1):
-        best = jnp.maximum(best, boxes[k, 0])
-    whole = stats[1] * jnp.exp(stats[0] - best)
+        best = jnp.maximum(best, boxes[k, 0:1, :])
+    whole = stats[1:2, :] * jnp.exp(stats[0:1, :] - best)
     for k in range(GROUPS - 1):
-        whole = whole + boxes[k, 1] * jnp.exp(boxes[k, 0] - best)
-    total[0] = best
-    total[1] = whole
+        whole = whole + boxes[k, 1:2, :] * jnp.exp(boxes[k, 0:1, :] - best)
+    total[...] = jnp.concatenate([best, whole, jnp.zeros((6, 128), jnp.float32)], axis=0)
     for copy in copies:
         copy.wait_send()
 
@@ -249,12 +275,12 @@
     vmem = pl.BlockSpec(memory_space=pltpu.VMEM)
     return pl.pallas_call(
         norm_kernel,
-        out_shape=jax.ShapeDtypeStruct((2, GROUPS * PART, 128), jnp.float32),
+        out_shape=jax.ShapeDtypeStruct((8, 128), jnp.float32),
         in_specs=[vmem],
         out_specs=vmem,
-        scratch_shapes=[pltpu.VMEM((GROUPS - 1, 2, GROUPS * PART, 128), jnp.float32),
+        scratch_shapes=[pltpu.VMEM((GROUPS - 1, 8, 128), jnp.float32),
                         pltpu.SemaphoreType.DMA((7,)), pltpu.SemaphoreType.DMA((7,))],
-        compiler_params=pltpu.CompilerParams(collective_id=2, has_side_effects=True),
+        compiler_params=pltpu.CompilerParams(collective_id=2, has_side_effects=True, vmem_limit_bytes=4 << 20),
         name="normalise",
     )(stats)
 
@@ -270,7 +296,9 @@
     @pl.when(table[slot * 8 + 5] > 0)
     def _():
         pid = table[slot * 8 + 6]
-        best, whole = total[0, pl.ds(pid, 1), :], total[1, pl.ds(pid, 1), :]
+        place = lax.broadcasted_iota(jnp.int32, (1, 128), 1) == pid
+        best = jnp.sum(jnp.where(place, total[0:1, :], 0.0), axis=1, keepdims=True)
+        whole = jnp.sum(jnp.where(place, total[1:2, :], 0.0), axis=1, keepdims=True)
         row, _, turn = lane_places(ACC_ROWS)
         later = turn >= row
         halves = []
@@ -332,7 +360,7 @@
         scratch_shapes=[pltpu.VMEM((CLS_LOC, ACC_ROWS, WIDTH), jnp.float32),
                         pltpu.VMEM((960, WIDTH), jnp.float32),
                         pltpu.VMEM((32, 128), jnp.float32)],
-        compiler_params=pltpu.CompilerParams(vmem_limit_bytes=40 << 20),
+        compiler_params=pltpu.CompilerParams(vmem_limit_bytes=28 << 20),
         name="sum_slots",
     )(table, total, scores, moved)
 
@@ -356,22 +384,27 @@
         copy.start()
         return copy
 
-    pending = []
     m1, m2, m3, m4, m5, m6 = {}, {}, {}, {}, {}, {}
-    for ch in range(NCH):
+    zm, zg, m7, m8, m9, m10 = {}, {}, {}, {}, {}, {}
+    masses = []
+
+    def far(ch):
         m1[ch] = send(p_ref.at[ch, yo, A], x1.at[ch], ysend.at[ch, 0], yrecv.at[ch, 0], up)
         m2[ch] = send(p_ref.at[ch, yo, B], x2.at[ch], ysend.at[ch, 1], yrecv.at[ch, 1], down)
+
+    def near(ch):
         m3[ch] = send(p_ref.at[ch, yp, B], d3.at[ch], ysend.at[ch, 2], yrecv.at[ch, 2], up)
         m4[ch] = send(p_ref.at[ch, ym, A], d4.at[ch], ysend.at[ch, 3], yrecv.at[ch, 3], down)
-    for ch in range(NCH):
+
+    def relay(ch):
         m1[ch].wait_recv()
         c1[ch] = (x1[ch].astype(jnp.float32) + p_ref[ch, yp, A].astype(jnp.float32)).astype(jnp.bfloat16)
         m5[ch] = send(c1.at[ch], e5.at[ch], ysend.at[ch, 4], yrecv.at[ch, 4], up)
         m2[ch].wait_recv()
         c2[ch] = (x2[ch].astype(jnp.float32) + p_ref[ch, ym, B].astype(jnp.float32)).astype(jnp.bfloat16)
         m6[ch] = send(c2.at[ch], e6.at[ch], ysend.at[ch, 5], yrecv.at[ch, 5], down)
-    zm = {}
-    for ch in range(NCH):
+
+    def column(ch):
         m4[ch].wait_recv()
         m5[ch].wait_recv()
         s_buf[ch, A] = (p_ref[ch, y, A].astype(jnp.float32) + e5[ch].astype(jnp.float32)
@@ -380,38 +413,50 @@
         m6[ch].wait_recv()
         s_buf[ch, B] = (p_ref[ch, y, B].astype(jnp.float32) + e6[ch].astype(jnp.float32)
                         + d3[ch].astype(jnp.float32)).astype(jnp.bfloat16)
-        for k in range(1, 8):
+        for k in (4, 3, 5, 2, 6, 1, 7):
             zm[ch, k] = send(s_buf.at[ch, (z + k) % 8], z_buf.at[ch, k - 1],
                              zsend.at[ch, k - 1], zrecv.at[ch, k - 1], zdev[k])
-    zg = {}
-    mass = None
-    for ch in range(NCH):
+
+    def finish(ch):
         num = s_buf[ch, z].astype(jnp.float32)
         for k in range(1, 8):
             zm[ch, k].wait_recv()
             num = num + z_buf[ch, k - 1].astype(jnp.float32)
         if ch == 0:
-            mass = num[0:1, :] + num[1:2, :] + 1.0
+            masses.append(num[0:1, :] + num[1:2, :] + 1.0)
+        mass = masses[0]
         place = DROWS * y + (ch * RC - LEAD) + lax.broadcasted_iota(jnp.int32, (RC, 128), 0)
         den = jnp.ones((RC, 128), jnp.float32)
         for c in range(CLS_LOC):
             here = (place >= c * ROTS) & (place < (c + 1) * ROTS)
             den = jnp.where(here, jnp.broadcast_to(mass[:, c:c + 1], (RC, 128)), den)
         g_ref[ch, y, z] = (num / den).astype(jnp.bfloat16)
-        for k in range(1, 8):
+        for k in (4, 3, 5, 2, 6, 1, 7):
             zg[ch, k] = send(g_ref.at[ch, y, z], g_ref.at[ch, y, z],
                              zsend.at[ch, 6 + k], zrecv.at[ch, 6 + k], zdev[k])
-    m7, m8, m9, m10 = {}, {}, {}, {}
-    for ch in range(NCH):
+
+    def share(ch):
         for k in range(1, 8):
             zg[ch, k].wait_recv()
         m7[ch] = send(g_ref.at[ch, y], g_ref.at[ch, y], ysend.at[ch, 6], yrecv.at[ch, 6], up)
         m8[ch] = send(g_ref.at[ch, y], g_ref.at[ch, y], ysend.at[ch, 7], yrecv.at[ch, 7], down)
-    for ch in range(NCH):
+
+    def pass_on(ch):
         m7[ch].wait_recv()
         m9[ch] = send(g_ref.at[ch, ym, A], g_ref.at[ch, ym, A], ysend.at[ch, 8], yrecv.at[ch, 8], up)
         m8[ch].wait_recv()
         m10[ch] = send(g_ref.at[ch, yp, B], g_ref.at[ch, yp, B], ysend.at[ch, 9], yrecv.at[ch, 9], down)
+
+    far(0)
+    near(0)
+    for step in range(NCH + 4):
+        if step + 1 < NCH:
+            far(step + 1)
+        for lag, stage in enumerate((relay, column, finish, share, pass_on)):
+            if stage is column and step + 1 < NCH:
+                near(step + 1)
+            if 0 <= step - lag < NCH:
+                stage(step - lag)
     for ch in range(NCH):
         m9[ch].wait_recv()
         m10[ch].wait_recv()
@@ -446,10 +491,8 @@
 
 
 def shards(particles, references, candidates, offsets):
-    meta = jnp.pad(jnp.concatenate([candidates, offsets], axis=1), ((0, 4), (0, 118)))
-    images, meta = gather_particles(particles.reshape(PART, 288, 128), meta)
-    refs = jnp.pad(references.reshape(CLS_LOC, ROTS, WIDTH)[:, ::-1], ((0, 0), (0, LHS_ROWS - ROTS), (0, 0)))
-    scores, moved, stats, table = score_slots(meta, jnp.asarray(unit_tables()), images, refs)
+    images, cands, priors, refs = gather_particles(particles.reshape(PART, 288, 128), candidates, offsets, references)
+    scores, moved, stats, table = score_slots(cands, priors, jnp.asarray(unit_tables()), images, refs)
     payload = sum_slots(table, normalise(stats), scores, moved)
     return unpack_average(reduce_average(payload))
 

time: 126 us -> 101 us (0.80); the launches traced: 124 us -> 101 us
  local copies, waits for them, and re-layouts: 22.2 us -> 7.03 us
  Pallas kernels: 101 us -> 93.9 us
    unnamed x12 -> x8, local copies, waits for them, and re-layouts: 9.73 us -> 4.16 us
    rev x1 -> x0, local copies, waits for them, and re-layouts: 5.13 us -> none  [shards(): references.reshape(CLS_LOC, ROTS, WIDTH)[:, ::-1]]
    reshape x1 -> x0, local copies, waits for them, and re-layouts: 4.09 us -> none  [shards(): references.reshape(CLS_LOC, ROTS, WIDTH)[:, ::-1]]
    pallas_call x1, Pallas kernels: 58.3 us -> 54.6 us  [reduce_average(): pl.pallas_call(reduce_kernel, out_shape=jax.ShapeDtypeStruct((NCH, 4, 8,...]
    pallas_call x1, Pallas kernels: 9.17 us -> 7.64 us  [normalise(): pl.pallas_call(norm_kernel, out_shape=jax.ShapeDtypeStruct((8, 128), jnp....]
    pallas_call x1, Pallas kernels: 10.7 us -> 9.37 us  [score_slots(): pl.pallas_call(score_kernel, grid=(SLOTS,), out_shape=(jax.ShapeDtypeStru...]
where the time goes in v3:
time: 101 us
  Pallas kernels  93.9 us (93%)
  local copies, waits for them, and re-layouts  7.03 us (7%)
    pallas_call x1, Pallas kernels, reduce_average(): pl.pallas_call(reduce_kernel, out_shape=jax.ShapeDtypeStruct((NCH, 4, 8,...  54.6 us
    pallas_call x1, Pallas kernels, gather_particles(): pl.pallas_call(gather_kernel, out_shape=(jax.ShapeDtypeStruct((GROUPS, PA...  16.7 us
    pallas_call x1, Pallas kernels, score_slots(): pl.pallas_call(score_kernel, grid=(SLOTS,), out_shape=(jax.ShapeDtypeStru...  9.37 us
    pallas_call x1, Pallas kernels, normalise(): pl.pallas_call(norm_kernel, out_shape=jax.ShapeDtypeStruct((8, 128), jnp....  7.64 us
    pallas_call x1, Pallas kernels, sum_slots(): pl.pallas_call(sum_kernel, grid=(SLOTS,), out_shape=jax.ShapeDtypeStruct(...  5.65 us
    unnamed x8, local copies, waits for them, and re-layouts  4.16 us
    reshape x1, local copies, waits for them, and re-layouts, unpack_average(): return rows.reshape(CLS_LOC, 36864)  2.24 us

profile of v3, /device:TPU:8, one launch (start us, length us, event | category | flops | bytes accessed | tf_op | source)
XLA Modules:
  0.0 101.0 jit_solution(14937058925598460744)
XLA Ops:
  0.0 0.0 copy-start.1
  0.0 0.8 copy.7.offs_ref
  0.8 1.0 copy.11
  1.8 0.0 copy-start
  1.8 1.7 %copy-done = bf16[25,36864]{1,0:T(8,128)(2,1)S(1)} copy-done((bf16[25,36864]{1,0:T(8,128)(2,1)S(1)}, bf16[25,36864]{1,0:T(8,128)(2,1)}, u32[]{:S(2)}) %copy-start) | copy-done | bytes 1843224
  3.5 0.0 copy-start.2
  3.5 0.7 copy-done.2
  4.2 16.7 %gather_particles.1 = (bf16[8,4,288,128]{3,2,1,0:T(8,128)(2,1)S(1)}, s32[8,4,8]{2,1,0:T(4,128)S(1)}, s32[8,4,2]{2,1,0:T(4,128)S(1)}, bf16[25,48,1024]{2,1,0:T(8,128)(2,1)S(1)}) custom-call(bf16[4,288,128]{2,1,0:T(8,128)(2,1)S(1)} %bitcast.9, s32[4,8]{1,0:T(4,128)S(1)} %copy-done.2, s32[4,2]{1,0:T(4,128)S(1)} %copy.7.offs_ref, bf16[25,36864]{1,0:T(8,128)(2,1)S(1)} %copy-done), custom_call_target="tpu_custom_call" | custom-call | tf_op jit(solution)/shard_map/gather_particles/pallas_call | solution.py:105
  20.9 0.0 copy-done.1
  20.9 9.4 %score_slots.1 = (f32[16,8,256]{2,1,0:T(8,128)S(1)}, bf16[16,256,1024]{2,1,0:T(8,128)(2,1)S(1)}, f32[8,128]{1,0:T(8,128)S(1)}, s32[136]{0:T(256)S(1)}) custom-call(s32[8,4,8]{2,1,0:T(4,128)S(1)} %get-tuple-element.13.cands, s32[8,4,2]{2,1,0:T(4,128)S(1)} %get-tuple-element.14.priors, f32[2,2,4,40,128]{4,3,2,1,0:T(8,128)S(1)} %copy-done.1, ...), custom_call_target="tpu_custom_call" | custom-call | tf_op jit(solution)/shard_map/score_slots/pallas_call | solution.py:231
  30.2 7.6 %normalise.1.total = f32[8,128]{1,0:T(8,128)S(1)} custom-call(f32[8,128]{1,0:T(8,128)S(1)} %get-tuple-element.18.stats), custom_call_target="tpu_custom_call" | custom-call | tf_op jit(solution)/shard_map/normalise/pallas_call | solution.py:276
  37.9 5.7 %sum_slots.1.p_ref = bf16[5,4,8,48,128]{4,3,2,1,0:T(8,128)(2,1)S(1)} custom-call(s32[136]{0:T(256)S(1)} %get-tuple-element.17.table, f32[8,128]{1,0:T(8,128)S(1)} %normalise.1.total, f32[16,8,256]{2,1,0:T(8,128)S(1)} %get-tuple-element.19.scores, bf16[16,256,1024]{2,1,0:T(8,128)(2,1)S(1)} %get-tuple-element.20.moved), custom_call_target="tpu_custom_call" | custom-call | tf_op jit(solution)/shard_map/sum_slots/pallas_call | solution.py:353
  43.6 54.6 %reduce_average.1 = bf16[5,4,8,48,128]{4,3,2,1,0:T(8,128)(2,1)S(1)} custom-call(bf16[5,4,8,48,128]{4,3,2,1,0:T(8,128)(2,1)S(1)} %sum_slots.1.p_ref), custom_call_target="tpu_custom_call" | custom-call | tf_op jit(solution)/shard_map/reduce_average/pallas_call | solution.py:470
  98.1 0.5 copy.8
  98.7 0.1 slice.4
  98.8 2.2 %reshape.11 = bf16[25,36864]{1,0:T(8,128)(2,1)} reshape(bf16[4,225,8,128]{3,2,1,0:T(8,128)(2,1)S(1)} %slice.4) | data formatting | bytes 3686400 | tf_op jit(solution)/shard_map/reshape | solution.py:490
Async XLA Ops:
  0.0 20.9 %copy-start.1 = (f32[2,2,4,40,128]{4,3,2,1,0:T(8,128)S(1)}, f32[2,2,4,40,128]{4,3,2,1,0:T(8,128)}, u32[]{:S(2)}) copy-start(f32[2,2,4,40,128]{4,3,2,1,0:T(8,128)} %constant.2.clone.unit) | copy-start | bytes 983044
  1.8 1.7 %copy-start = (bf16[25,36864]{1,0:T(8,128)(2,1)S(1)}, bf16[25,36864]{1,0:T(8,128)(2,1)}, u32[]{:S(2)}) copy-start(bf16[25,36864]{1,0:T(8,128)(2,1)} %refs_ref.1) | copy-start | bytes 5529604
  3.5 0.7 copy-start.2

commit v4 on v3

--- a/solution.py
+++ b/solution.py
@@ -25,7 +25,7 @@
     return out.astype(np.float32)
 
 
-def gather_kernel(p_ref, cand_ref, offs_ref, refs_ref, out_ref, cout_ref, oout_ref, rows_ref, tall, lsem, ssem, rsem):
+def gather_kernel(p_ref, cand_ref, offs_ref, refs_ref, unit, out_ref, cout_ref, oout_ref, rows_ref, powers, flat, tall, lsem, ssem, rsem):
     me = lax.axis_index("cls")
     core = me % 2
     right, left, across = (me + 2) % GROUPS, (me + 6) % GROUPS, (me + 4) % GROUPS
@@ -55,6 +55,8 @@
     locals_ = [pltpu.make_async_copy(p_ref, out_ref.at[me], lsem.at[0]),
                pltpu.make_async_copy(cand_ref, cout_ref.at[me], lsem.at[1]),
                pltpu.make_async_copy(offs_ref, oout_ref.at[me], lsem.at[2])]
+    fetch = pltpu.make_async_copy(refs_ref, flat, lsem.at[3])
+    fetch.start()
     for copy in locals_:
         copy.start()
 
@@ -64,7 +66,7 @@
         return carry
 
     def spread(l, carry):
-        value = refs_ref[:, pl.ds(pl.multiple_of(l * WIDTH, WIDTH), WIDTH)].astype(jnp.float32)
+        value = flat[:, pl.ds(pl.multiple_of(l * WIDTH, WIDTH), WIDTH)].astype(jnp.float32)
         for g in range(8):
             tall[g, pl.ds(ROTS - 1 - l, CLS_LOC, stride=LHS_ROWS), :] = value[:, 128 * g:128 * g + 128]
         return carry
@@ -76,6 +78,7 @@
         return carry
 
     lax.fori_loop(0, CLS_LOC, clear, 0)
+    fetch.wait()
     lax.fori_loop(0, ROTS, spread, 0)
     r0.wait_recv()
     fr = send(out_ref.at[left, h0], out_ref.at[left, h0], 5, right)
@@ -84,6 +87,15 @@
     fl = send(out_ref.at[right, h1], out_ref.at[right, h1], 6, left)
     s1 = send(out_ref.at[right, h1], out_ref.at[right, h1], 8, pair)
     lax.fori_loop(0, CLS_LOC, pack, 0)
+    for axis in range(2):
+        powers[axis, 0, 0] = jnp.ones((4, ACC_ROWS, 128), jnp.float32)
+        powers[axis, 0, 1] = jnp.zeros((4, ACC_ROWS, 128), jnp.float32)
+        powers[axis, 1] = unit[axis]
+        for t in range(2, 8):
+            pc, ps = powers[axis, t - 1, 0], powers[axis, t - 1, 1]
+            qc, qs = unit[axis, 0], unit[axis, 1]
+            powers[axis, t, 0] = pc * qc - ps * qs
+            powers[axis, t, 1] = ps * qc + pc * qs
     r1.wait_recv()
     s2 = send(out_ref.at[left, h1], out_ref.at[left, h1], 9, pair)
     l0.wait_recv()
@@ -100,21 +112,22 @@
         copy.wait_send()
 
 
-def gather_particles(images, candidates, offsets, refs):
+def gather_particles(images, candidates, offsets, refs, unit):
     vmem = pl.BlockSpec(memory_space=pltpu.VMEM)
     return pl.pallas_call(
         gather_kernel,
         out_shape=(jax.ShapeDtypeStruct((GROUPS, PART, 288, 128), jnp.bfloat16),
                    jax.ShapeDtypeStruct((GROUPS, PART, 8), jnp.int32),
-                   jax.ShapeDtypeStruct((GROUPS, PART, 2), jnp.int32),
-                   jax.ShapeDtypeStruct((CLS_LOC, LHS_ROWS, WIDTH), jnp.bfloat16)),
-        in_specs=[vmem] * 4,
-        out_specs=(vmem,) * 4,
-        scratch_shapes=[pltpu.VMEM((8, CLS_LOC * LHS_ROWS, 128), jnp.float32), pltpu.SemaphoreType.DMA((3,)),
+                   jax.ShapeDtypeStruct((GROUPS, 2, PART), jnp.int32),
+                   jax.ShapeDtypeStruct((CLS_LOC, LHS_ROWS, WIDTH), jnp.bfloat16),
+                   jax.ShapeDtypeStruct((2, 8, 2, 4, ACC_ROWS, 128), jnp.float32)),
+        in_specs=[vmem] + [pl.BlockSpec(memory_space=pltpu.HBM)] * 3 + [vmem],
+        out_specs=(vmem,) * 5,
+        scratch_shapes=[pltpu.VMEM((CLS_LOC, ROTS * WIDTH), jnp.bfloat16), pltpu.VMEM((8, CLS_LOC * LHS_ROWS, 128), jnp.float32), pltpu.SemaphoreType.DMA((4,)),
                         pltpu.SemaphoreType.DMA((27,)), pltpu.SemaphoreType.DMA((27,))],
         compiler_params=pltpu.CompilerParams(collective_id=1, has_side_effects=True, vmem_limit_bytes=24 << 20),
         name="gather_particles",
-    )(images, candidates, offsets, refs)
+    )(images, candidates, offsets, refs, unit)
 
 
 def group_turn(lane):
@@ -127,48 +140,27 @@
     return row, lane, group_turn(lane)
 
 
-def score_kernel(cands, priors, unit, images, refs, scores, moved, stats, table, wide, powers):
-    slot = pl.program_id(0)
+def score_kernel(cands, priors, powers, images, refs, scores, moved, stats, table, wide):
     owner = lax.axis_index("cls")
-
-    @pl.when(slot == 0)
-    def _():
-        for v in range(GROUPS):
-            table[2 * v * 8 + 5] = 0
-            table[(2 * v + 1) * 8 + 5] = 0
-            place = jnp.int32(2 * v)
-            for i in range(PART):
-                k = jnp.int32(0)
-                for t in range(8):
-                    c = cands[v, i, t] - owner * CLS_LOC
-                    table[place * 8 + k] = c
-                    k = k + jnp.where((c >= 0) & (c < CLS_LOC), 1, 0)
-                hit = jnp.where(k > 0, 1, 0)
-
-                @pl.when(hit > 0)
-                def _():
-                    table[place * 8 + 5] = 1
-                    table[place * 8 + 6] = PART * v + i
-
-                place = place + hit
-        wide[288:320, :] = jnp.zeros((32, 128), jnp.float32)
-        for axis in range(2):
-            powers[axis, 0, 0] = jnp.ones((4, ACC_ROWS, 128), jnp.float32)
-            powers[axis, 0, 1] = jnp.zeros((4, ACC_ROWS, 128), jnp.float32)
-            powers[axis, 1] = unit[axis]
-            for t in range(2, 8):
-                c0, s0 = powers[axis, t - 1, 0], powers[axis, t - 1, 1]
-                c1, s1 = unit[axis, 0], unit[axis, 1]
-                powers[axis, t, 0] = c0 * c1 - s0 * s1
-                powers[axis, t, 1] = s0 * c1 + c0 * s1
-        first = lax.broadcasted_iota(jnp.int32, (8, 128), 0) == 0
-        stats[...] = jnp.where(first, NEGATIVE, 0.0)
-
-    @pl.when(table[slot * 8 + 5] > 0)
-    def _():
+    base = jnp.int32(0)
+    for pid in range(GROUPS * PART):
+        spot = base
+        for t in range(8):
+            c = cands[pid // PART, pid % PART, t] - owner * CLS_LOC
+            table[spot] = c
+            spot = spot + jnp.where(c.astype(jnp.uint32) < CLS_LOC, 1, 0)
+        table[base + 6] = pid
+        base = base + jnp.where(spot > base, 8, 0)
+    place = base // 8
+    table[SLOTS * 8 + 7] = place
+    wide[288:320, :] = jnp.zeros((32, 128), jnp.float32)
+    first = lax.broadcasted_iota(jnp.int32, (8, 128), 0) == 0
+    stats[...] = jnp.where(first, NEGATIVE, 0.0)
+
+    def one_slot(slot, carry):
         pid = table[slot * 8 + 6]
         v, i = pid // PART, pid % PART
-        tx, ty = priors[v, i, 0], priors[v, i, 1]
+        tx, ty = priors[v, 0, i], priors[v, 1, i]
         ax, ay = jnp.abs(tx), jnp.abs(ty)
         gx = jnp.where(tx < 0, -1.0, 1.0).astype(jnp.float32)
         gy = jnp.where(ty < 0, -1.0, 1.0).astype(jnp.float32)
@@ -183,16 +175,16 @@
             zr, zi = re * bc + im * bs, im * bc - re * bs
             real, imag = [zr], [zi]
             for axis in range(2):
-                uc, us = unit[axis, 0, a], unit[axis, 1, a]
+                uc, us = powers[axis, 1, 0, a], powers[axis, 1, 1, a]
                 rc, rs, ic, js = zr * uc, zr * us, zi * uc, zi * us
                 real += [rc + js, rc - js]
                 imag += [ic - rs, ic + rs]
             for m, part in enumerate((real, imag)):
                 lanes = pl.ds(256 * a + 128 * m, 128)
-                moved[0, 0:128, lanes] = jnp.concatenate(part[0:3] + [gap8], axis=0).astype(jnp.bfloat16)
-                moved[0, 128:256, lanes] = jnp.concatenate(part[3:5] + [gap48], axis=0).astype(jnp.bfloat16)
+                moved[slot, 0:128, lanes] = jnp.concatenate(part[0:3] + [gap8], axis=0).astype(jnp.bfloat16)
+                moved[slot, 128:256, lanes] = jnp.concatenate(part[3:5] + [gap48], axis=0).astype(jnp.bfloat16)
         lhs = jnp.concatenate([refs[table[slot * 8 + k]] for k in range(4)], axis=0)
-        pairs = lax.dot_general(lhs, moved[0], (((1,), (1,)), ((), ())), preferred_element_type=jnp.float32)
+        pairs = lax.dot_general(lhs, moved[slot], (((1,), (1,)), ((), ())), preferred_element_type=jnp.float32)
         row = lax.broadcasted_iota(jnp.int32, (ACC_ROWS, 128), 0)
         lane = lax.broadcasted_iota(jnp.int32, (ACC_ROWS, 128), 1)
         turn = group_turn(jnp.where(lane >= ROTS - 1, lane - (ROTS - 1), lane + 128 - (ROTS - 1)))
@@ -216,33 +208,33 @@
             row8 = lax.broadcasted_iota(jnp.int32, (8, 128), 0)
             good = (turn1 < ROTS) & (lane1 < (120 if half == 0 else 80)) & (row8 < 4)
             line = jnp.where(good, whole, NEGATIVE)
-            scores[0, :, 128 * half:128 * half + 128] = line
+            scores[slot, :, 128 * half:128 * half + 128] = line
             lines.append(line)
         best = jnp.max(jnp.max(jnp.maximum(lines[0], lines[1]), axis=1, keepdims=True), axis=0, keepdims=True)
         power = jnp.exp(lines[0] - best) + jnp.exp(lines[1] - best)
         mass = jnp.sum(jnp.sum(power, axis=1, keepdims=True), axis=0, keepdims=True)
-        place = lax.broadcasted_iota(jnp.int32, (1, 128), 1) == pid
-        stats[0:1, :] = jnp.where(place, best, stats[0:1, :])
-        stats[1:2, :] = jnp.where(place, mass, stats[1:2, :])
-
-
-def score_slots(cands, priors, unit, images, refs):
+        here = lax.broadcasted_iota(jnp.int32, (1, 128), 1) == pid
+        stats[0:1, :] = jnp.where(here, best, stats[0:1, :])
+        stats[1:2, :] = jnp.where(here, mass, stats[1:2, :])
+        return carry
+
+    lax.fori_loop(0, place, one_slot, 0)
+
+
+def score_slots(cands, priors, powers, images, refs):
     vmem, smem = pl.BlockSpec(memory_space=pltpu.VMEM), pl.BlockSpec(memory_space=pltpu.SMEM)
     return pl.pallas_call(
         score_kernel,
-        grid=(SLOTS,),
         out_shape=(jax.ShapeDtypeStruct((SLOTS, 8, 256), jnp.float32),
                    jax.ShapeDtypeStruct((SLOTS, 256, WIDTH), jnp.bfloat16),
                    jax.ShapeDtypeStruct((8, 128), jnp.float32),
-                   jax.ShapeDtypeStruct((17 * 8,), jnp.int32)),
+                   jax.ShapeDtypeStruct(((SLOTS + 1) * 8,), jnp.int32)),
         in_specs=[smem, smem, vmem, vmem, vmem],
-        out_specs=(pl.BlockSpec((1, 8, 256), lambda i: (i, 0, 0)),
-                   pl.BlockSpec((1, 256, WIDTH), lambda i: (i, 0, 0)), vmem, smem),
-        scratch_shapes=[pltpu.VMEM((320, 128), jnp.float32),
-                        pltpu.VMEM((2, 8, 2, 4, ACC_ROWS, 128), jnp.float32)],
-        compiler_params=pltpu.CompilerParams(vmem_limit_bytes=28 << 20),
+        out_specs=(vmem, vmem, vmem, smem),
+        scratch_shapes=[pltpu.VMEM((320, 128), jnp.float32)],
+        compiler_params=pltpu.CompilerParams(vmem_limit_bytes=32 << 20),
         name="score_slots",
-    )(cands, priors, unit, images, refs)
+    )(cands, priors, powers, images, refs)
 
 
 def norm_kernel(stats, total, boxes, ssem, rsem):
@@ -285,16 +277,12 @@
     )(stats)
 
 
-def sum_kernel(table, total, scores, moved, out, acc, comp, masses):
-    slot = pl.program_id(0)
-
-    @pl.when(slot == 0)
-    def _():
-        acc[...] = jnp.zeros(acc.shape, jnp.float32)
-        masses[...] = jnp.zeros(masses.shape, jnp.float32)
-
-    @pl.when(table[slot * 8 + 5] > 0)
-    def _():
+def sum_kernel(table, total, scores, moved, out, acc, comp, masses, spread):
+    filled = table[SLOTS * 8 + 7]
+    acc[...] = jnp.zeros(acc.shape, jnp.float32)
+    masses[...] = jnp.zeros(masses.shape, jnp.float32)
+
+    def prepare(slot, count):
         pid = table[slot * 8 + 6]
         place = lax.broadcasted_iota(jnp.int32, (1, 128), 1) == pid
         best = jnp.sum(jnp.where(place, total[0:1, :], 0.0), axis=1, keepdims=True)
@@ -304,7 +292,7 @@
         halves = []
         mass = jnp.zeros((8, 1), jnp.float32)
         for half in range(2):
-            weight = jnp.exp(scores[0, :, 128 * half:128 * half + 128] - best) / whole
+            weight = jnp.exp(scores[slot, :, 128 * half:128 * half + 128] - best) / whole
             weight = weight.astype(jnp.bfloat16).astype(jnp.float32)
             mass = mass + jnp.sum(weight, axis=1, keepdims=True)
             back = pltpu.roll(weight, 92, 1)
@@ -315,52 +303,58 @@
                 rows.append(jnp.where(later, pltpu.roll(one, 0, 1, stride=1, stride_axis=0),
                                       pltpu.roll(two, 0, 1, stride=1, stride_axis=0)))
             halves.append(jnp.concatenate(rows, axis=0))
-        spread = jnp.concatenate(halves, axis=1).astype(jnp.bfloat16)
+        spread[slot % 2] = jnp.concatenate(halves, axis=1).astype(jnp.bfloat16)
         for k in range(4):
             c = table[slot * 8 + k]
-            masses[pl.ds(c, 1), :] = masses[pl.ds(c, 1), :] + jnp.broadcast_to(mass[k:k + 1, :], (1, 128))
-        contrib = jnp.dot(spread, moved[0], preferred_element_type=jnp.float32)
+            masses[pl.ds(c, 1), :] = masses[pl.ds(c, 1), :] + count * jnp.broadcast_to(mass[k:k + 1, :], (1, 128))
+
+    def one_slot(slot, carry):
+        contrib = jnp.dot(spread[slot % 2], moved[slot], preferred_element_type=jnp.float32)
+        prepare(jnp.minimum(slot + 1, filled - 1), jnp.where(slot + 1 < filled, 1.0, 0.0))
         for k in range(4):
             c = table[slot * 8 + k]
             acc[c] = acc[c] + contrib[ACC_ROWS * k:ACC_ROWS * (k + 1)]
-
-    @pl.when(slot == SLOTS - 1)
+        return carry
+
+    @pl.when(filled > 0)
     def _():
-        row = lax.broadcasted_iota(jnp.int32, (32, 128), 0)
-        lane = lax.broadcasted_iota(jnp.int32, (32, 128), 1)
-        line = jnp.sum(jnp.where(row == lane, masses[...], 0.0), axis=0, keepdims=True)
-        high = line.astype(jnp.bfloat16).astype(jnp.float32)
-        lead = jnp.concatenate([high, line - high, jnp.zeros((14, 128), jnp.float32)], axis=0)
+        prepare(0, 1.0)
+        lax.fori_loop(0, filled, one_slot, 0)
+
+    row = lax.broadcasted_iota(jnp.int32, (32, 128), 0)
+    lane = lax.broadcasted_iota(jnp.int32, (32, 128), 1)
+    line = jnp.sum(jnp.where(row == lane, masses[...], 0.0), axis=0, keepdims=True)
+    high = line.astype(jnp.bfloat16).astype(jnp.float32)
+    lead = jnp.concatenate([high, line - high, jnp.zeros((14, 128), jnp.float32)], axis=0)
+    for y in range(4):
+        comp[y * 240:y * 240 + 16, :] = jnp.concatenate([lead] * 8, axis=1)
+    for c in range(CLS_LOC):
+        start = c * ROTS
+        while start < (c + 1) * ROTS:
+            y = start // DROWS
+            stop = min((c + 1) * ROTS, (y + 1) * DROWS)
+            to = y * 240 + LEAD + start - y * DROWS
+            comp[to:to + stop - start, :] = acc[c, start - c * ROTS:stop - c * ROTS, :]
+            start = stop
+    for ch in range(NCH):
         for y in range(4):
-            comp[y * 240:y * 240 + 16, :] = jnp.concatenate([lead] * 8, axis=1)
-        for c in range(CLS_LOC):
-            start = c * ROTS
-            while start < (c + 1) * ROTS:
-                y = start // DROWS
-                stop = min((c + 1) * ROTS, (y + 1) * DROWS)
-                to = y * 240 + LEAD + start - y * DROWS
-                comp[to:to + stop - start, :] = acc[c, start - c * ROTS:stop - c * ROTS, :]
-                start = stop
-        for ch in range(NCH):
-            for y in range(4):
-                for z in range(8):
-                    out[ch, y, z] = comp[y * 240 + ch * RC:y * 240 + (ch + 1) * RC,
-                                         128 * z:128 * z + 128].astype(jnp.bfloat16)
+            for z in range(8):
+                out[ch, y, z] = comp[y * 240 + ch * RC:y * 240 + (ch + 1) * RC,
+                                     128 * z:128 * z + 128].astype(jnp.bfloat16)
 
 
 def sum_slots(table, total, scores, moved):
     vmem, smem = pl.BlockSpec(memory_space=pltpu.VMEM), pl.BlockSpec(memory_space=pltpu.SMEM)
     return pl.pallas_call(
         sum_kernel,
-        grid=(SLOTS,),
         out_shape=jax.ShapeDtypeStruct((NCH, 4, 8, RC, 128), jnp.bfloat16),
-        in_specs=[smem, vmem, pl.BlockSpec((1, 8, 256), lambda i: (i, 0, 0)),
-                  pl.BlockSpec((1, 256, WIDTH), lambda i: (i, 0, 0))],
+        in_specs=[smem, vmem, vmem, vmem],
         out_specs=vmem,
         scratch_shapes=[pltpu.VMEM((CLS_LOC, ACC_ROWS, WIDTH), jnp.float32),
                         pltpu.VMEM((960, WIDTH), jnp.float32),
-                        pltpu.VMEM((32, 128), jnp.float32)],
-        compiler_params=pltpu.CompilerParams(vmem_limit_bytes=28 << 20),
+                        pltpu.VMEM((32, 128), jnp.float32),
+                        pltpu.VMEM((2, 4 * ACC_ROWS, 256), jnp.bfloat16)],
+        compiler_params=pltpu.CompilerParams(vmem_limit_bytes=32 << 20),
         name="sum_slots",
     )(table, total, scores, moved)
 
@@ -490,9 +484,15 @@
     return rows.reshape(CLS_LOC, 36864)
 
 
+def in_hbm(*arrays):
+    return [pltpu.with_memory_space_constraint(array, pltpu.HBM) for array in arrays]
+
+
 def shards(particles, references, candidates, offsets):
-    images, cands, priors, refs = gather_particles(particles.reshape(PART, 288, 128), candidates, offsets, references)
-    scores, moved, stats, table = score_slots(cands, priors, jnp.asarray(unit_tables()), images, refs)
+    unit = jnp.asarray(unit_tables())
+    images, cands, priors, refs, powers = gather_particles(
+        particles.reshape(PART, 288, 128), *in_hbm(candidates, offsets.T, references), unit)
+    scores, moved, stats, table = score_slots(cands, priors, powers, images, refs)
     payload = sum_slots(table, normalise(stats), scores, moved)
     return unpack_average(reduce_average(payload))
 

time: 101 us -> 95.4 us (0.945)
  Pallas kernels: 93.9 us -> 89.9 us
  local copies, waits for them, and re-layouts: 7.03 us -> 4.84 us
    unnamed x8 -> x3, local copies, waits for them, and re-layouts: 4.16 us -> 1.97 us
    pallas_call x1, Pallas kernels: 54.6 us -> 52.5 us  [reduce_average(): pl.pallas_call(reduce_kernel, out_shape=jax.ShapeDtypeStruct((NCH, 4, 8,...]
    pallas_call x2, Pallas kernels: 15 us -> 13.6 us  [the longest x1 8.9 us: score_slots(): pl.pallas_call(score_kernel, out_shape=(jax.ShapeDtypeStruct((SLOTS, 8, 2...]
where the time goes in v4:
time: 95.4 us; the launch traced here: 94.8 us
  Pallas kernels  89.9 us (94%)
  local copies, waits for them, and re-layouts  4.84 us (5%)
    pallas_call x1, Pallas kernels, reduce_average(): pl.pallas_call(reduce_kernel, out_shape=jax.ShapeDtypeStruct((NCH, 4, 8,...  52.5 us
    pallas_call x1, Pallas kernels, gather_particles(): pl.pallas_call(gather_kernel, out_shape=(jax.ShapeDtypeStruct((GROUPS, PA...  16.8 us
    pallas_call x1, Pallas kernels, score_slots(): pl.pallas_call(score_kernel, out_shape=(jax.ShapeDtypeStruct((SLOTS, 8, 2...  8.9 us
    pallas_call x1, Pallas kernels, normalise(): pl.pallas_call(norm_kernel, out_shape=jax.ShapeDtypeStruct((8, 128), jnp....  7.02 us
    pallas_call x1, Pallas kernels, sum_slots(): pl.pallas_call(sum_kernel, out_shape=jax.ShapeDtypeStruct((NCH, 4, 8, RC,...  4.67 us
    reshape x1, local copies, waits for them, and re-layouts, unpack_average(): return rows.reshape(CLS_LOC, 36864)  2.24 us
    unnamed x3, local copies, waits for them, and re-layouts  1.97 us

profile of v4, /device:TPU:8, one launch (start us, length us, event | category | flops | bytes accessed | tf_op | source)
XLA Modules:
  0.0 94.8 jit_solution(5420613409973278813)
XLA Ops:
  0.0 1.0 %copy.9 = bf16[1,4,288,128]{3,2,1,0:T(8,128)(2,1)S(1)} copy(bf16[1,4,288,128]{3,1,2,0:T(4,128)(2,1)} %bitcast.12) | data formatting | bytes 589824
  1.0 0.0 copy-start
  1.0 1.0 %copy-done = f32[2,2,4,40,128]{4,3,2,1,0:T(8,128)S(1)} copy-done((f32[2,2,4,40,128]{4,3,2,1,0:T(8,128)S(1)}, f32[2,2,4,40,128]{4,3,2,1,0:T(8,128)}, u32[]{:S(2)}) %copy-start) | copy-done | bytes 327704
  2.0 16.8 %gather_particles.1 = (bf16[8,4,288,128]{3,2,1,0:T(8,128)(2,1)S(1)}, s32[8,4,8]{2,1,0:T(4,128)S(1)}, s32[8,2,4]{2,1,0:T(2,128)S(1)}, bf16[25,48,1024]{2,1,0:T(8,128)(2,1)S(1)}, f32[2,8,2,4,40,128]{5,4,3,2,1,0:T(8,128)S(1)}) custom-call(bf16[4,288,128]{2,1,0:T(8,128)(2,1)S(1)} %bitcast.10, s32[4,8]{1,0:T(4,128)} %cand_ref.1, s32[2,4]{1,0:T(2,128)} %bitcast.13, ...), custom_call_target="tpu_custom_call" | custom-call | tf_op jit(solution)/shard_map/gather_particles/pallas_call | solution.py:117
  18.8 8.9 %score_slots.1 = (f32[16,8,256]{2,1,0:T(8,128)S(1)}, bf16[16,256,1024]{2,1,0:T(8,128)(2,1)S(1)}, f32[8,128]{1,0:T(8,128)S(1)}, s32[136]{0:T(256)S(1)}) custom-call(s32[8,4,8]{2,1,0:T(4,128)S(1)} %get-tuple-element.14.cands, s32[8,2,4]{2,1,0:T(2,128)S(1)} %get-tuple-element.15.priors, f32[2,8,2,4,40,128]{5,4,3,2,1,0:T(8,128)S(1)} %get-tuple-element.16.powers, ...), custom_call_target="tpu_custom_call" | custom-call | tf_op jit(solution)/shard_map/score_slots/pallas_call | solution.py:226
  27.7 7.0 %normalise.1.total = f32[8,128]{1,0:T(8,128)S(1)} custom-call(f32[8,128]{1,0:T(8,128)S(1)} %get-tuple-element.20.stats), custom_call_target="tpu_custom_call" | custom-call | tf_op jit(solution)/shard_map/normalise/pallas_call | solution.py:268
  34.8 4.7 %sum_slots.1.p_ref = bf16[5,4,8,48,128]{4,3,2,1,0:T(8,128)(2,1)S(1)} custom-call(s32[136]{0:T(256)S(1)} %get-tuple-element.19.table, f32[8,128]{1,0:T(8,128)S(1)} %normalise.1.total, f32[16,8,256]{2,1,0:T(8,128)S(1)} %get-tuple-element.21.scores, bf16[16,256,1024]{2,1,0:T(8,128)(2,1)S(1)} %get-tuple-element.22.moved), custom_call_target="tpu_custom_call" | custom-call | tf_op jit(solution)/shard_map/sum_slots/pallas_call | solution.py:348
  39.4 52.5 %reduce_average.1 = bf16[5,4,8,48,128]{4,3,2,1,0:T(8,128)(2,1)S(1)} custom-call(bf16[5,4,8,48,128]{4,3,2,1,0:T(8,128)(2,1)S(1)} %sum_slots.1.p_ref), custom_call_target="tpu_custom_call" | custom-call | tf_op jit(solution)/shard_map/reduce_average/pallas_call | solution.py:464
  91.9 0.5 copy.6
  92.5 0.1 slice.4
  92.6 2.2 %reshape.11 = bf16[25,36864]{1,0:T(8,128)(2,1)} reshape(bf16[4,225,8,128]{3,2,1,0:T(8,128)(2,1)S(1)} %slice.4) | data formatting | bytes 3686400 | tf_op jit(solution)/shard_map/reshape | solution.py:484
Async XLA Ops:
  1.0 1.0 %copy-start = (f32[2,2,4,40,128]{4,3,2,1,0:T(8,128)S(1)}, f32[2,2,4,40,128]{4,3,2,1,0:T(8,128)}, u32[]{:S(2)}) copy-start(f32[2,2,4,40,128]{4,3,2,1,0:T(8,128)} %constant.2.clone.unit) | copy-start | bytes 983044

commit v5 on v4

--- a/solution.py
+++ b/solution.py
@@ -25,7 +25,7 @@
     return out.astype(np.float32)
 
 
-def gather_kernel(p_ref, cand_ref, offs_ref, refs_ref, unit, out_ref, cout_ref, oout_ref, rows_ref, powers, flat, tall, lsem, ssem, rsem):
+def gather_kernel(p_ref, cand_ref, offs_ref, refs_ref, unit_ref, out_ref, cout_ref, oout_ref, rows_ref, powers, flat, unit, tall, lsem, ssem, rsem):
     me = lax.axis_index("cls")
     core = me % 2
     right, left, across = (me + 2) % GROUPS, (me + 6) % GROUPS, (me + 4) % GROUPS
@@ -57,6 +57,8 @@
                pltpu.make_async_copy(offs_ref, oout_ref.at[me], lsem.at[2])]
     fetch = pltpu.make_async_copy(refs_ref, flat, lsem.at[3])
     fetch.start()
+    fetch_unit = pltpu.make_async_copy(unit_ref, unit, lsem.at[4])
+    fetch_unit.start()
     for copy in locals_:
         copy.start()
 
@@ -87,6 +89,7 @@
     fl = send(out_ref.at[right, h1], out_ref.at[right, h1], 6, left)
     s1 = send(out_ref.at[right, h1], out_ref.at[right, h1], 8, pair)
     lax.fori_loop(0, CLS_LOC, pack, 0)
+    fetch_unit.wait()
     for axis in range(2):
         powers[axis, 0, 0] = jnp.ones((4, ACC_ROWS, 128), jnp.float32)
         powers[axis, 0, 1] = jnp.zeros((4, ACC_ROWS, 128), jnp.float32)
@@ -121,9 +124,10 @@
                    jax.ShapeDtypeStruct((GROUPS, 2, PART), jnp.int32),
                    jax.ShapeDtypeStruct((CLS_LOC, LHS_ROWS, WIDTH), jnp.bfloat16),
                    jax.ShapeDtypeStruct((2, 8, 2, 4, ACC_ROWS, 128), jnp.float32)),
-        in_specs=[vmem] + [pl.BlockSpec(memory_space=pltpu.HBM)] * 3 + [vmem],
+        in_specs=[vmem] + [pl.BlockSpec(memory_space=pltpu.HBM)] * 4,
         out_specs=(vmem,) * 5,
-        scratch_shapes=[pltpu.VMEM((CLS_LOC, ROTS * WIDTH), jnp.bfloat16), pltpu.VMEM((8, CLS_LOC * LHS_ROWS, 128), jnp.float32), pltpu.SemaphoreType.DMA((4,)),
+        scratch_shapes=[pltpu.VMEM((CLS_LOC, ROTS * WIDTH), jnp.bfloat16),
+                        pltpu.VMEM((2, 2, 4, ACC_ROWS, 128), jnp.float32), pltpu.VMEM((8, CLS_LOC * LHS_ROWS, 128), jnp.float32), pltpu.SemaphoreType.DMA((5,)),
                         pltpu.SemaphoreType.DMA((27,)), pltpu.SemaphoreType.DMA((27,))],
         compiler_params=pltpu.CompilerParams(collective_id=1, has_side_effects=True, vmem_limit_bytes=24 << 20),
         name="gather_particles",
@@ -425,12 +429,26 @@
             here = (place >= c * ROTS) & (place < (c + 1) * ROTS)
             den = jnp.where(here, jnp.broadcast_to(mass[:, c:c + 1], (RC, 128)), den)
         g_ref[ch, y, z] = (num / den).astype(jnp.bfloat16)
-        for k in (4, 3, 5, 2, 6, 1, 7):
-            zg[ch, k] = send(g_ref.at[ch, y, z], g_ref.at[ch, y, z],
-                             zsend.at[ch, 6 + k], zrecv.at[ch, 6 + k], zdev[k])
+        for k in (2, 6, 1, 7):
+            hand(ch, k, z, k)
+
+    def hand(ch, k, piece, to):
+        zg[ch, k] = send(g_ref.at[ch, y, piece], g_ref.at[ch, y, piece],
+                         zsend.at[ch, 6 + k], zrecv.at[ch, 6 + k], zdev[to])
+
+    def forward(ch):
+        below, above = (z + 6) % 8, (z + 2) % 8
+        zg[ch, 2].wait_recv()
+        if ch % 2 == 0:
+            hand(ch, 4, below, 2)
+        hand(ch, 3, below, 1)
+        zg[ch, 6].wait_recv()
+        if ch % 2 == 1:
+            hand(ch, 4, above, 6)
+        hand(ch, 5, above, 7)
 
     def share(ch):
-        for k in range(1, 8):
+        for k in (1, 7, 3, 4, 5):
             zg[ch, k].wait_recv()
         m7[ch] = send(g_ref.at[ch, y], g_ref.at[ch, y], ysend.at[ch, 6], yrecv.at[ch, 6], up)
         m8[ch] = send(g_ref.at[ch, y], g_ref.at[ch, y], ysend.at[ch, 7], yrecv.at[ch, 7], down)
@@ -443,10 +461,10 @@
 
     far(0)
     near(0)
-    for step in range(NCH + 4):
+    for step in range(NCH + 5):
         if step + 1 < NCH:
             far(step + 1)
-        for lag, stage in enumerate((relay, column, finish, share, pass_on)):
+        for lag, stage in enumerate((relay, column, finish, forward, share, pass_on)):
             if stage is column and step + 1 < NCH:
                 near(step + 1)
             if 0 <= step - lag < NCH:
@@ -491,7 +509,7 @@
 def shards(particles, references, candidates, offsets):
     unit = jnp.asarray(unit_tables())
     images, cands, priors, refs, powers = gather_particles(
-        particles.reshape(PART, 288, 128), *in_hbm(candidates, offsets.T, references), unit)
+        particles.reshape(PART, 288, 128), *in_hbm(candidates, offsets.T, references, unit))
     scores, moved, stats, table = score_slots(cands, priors, powers, images, refs)
     payload = sum_slots(table, normalise(stats), scores, moved)
     return unpack_average(reduce_average(payload))

time: 95.4 us -> 93.9 us (0.984); the launches traced: 94.8 us -> 94.3 us
  local copies, waits for them, and re-layouts: 4.84 us -> 3.87 us
    pallas_call x1, Pallas kernels: 7.02 us -> 8.53 us  [normalise(): pl.pallas_call(norm_kernel, out_shape=jax.ShapeDtypeStruct((8, 128), jnp....]
    unnamed x3 -> x1, local copies, waits for them, and re-layouts: 1.97 us -> 1 us
where the time goes in v5:
time: 93.9 us; the launch traced here: 94.3 us
  Pallas kernels  90.4 us (96%)
  local copies, waits for them, and re-layouts  3.87 us (4%)
    pallas_call x1, Pallas kernels, reduce_average(): pl.pallas_call(reduce_kernel, out_shape=jax.ShapeDtypeStruct((NCH, 4, 8,...  52.3 us
    pallas_call x1, Pallas kernels, gather_particles(): pl.pallas_call(gather_kernel, out_shape=(jax.ShapeDtypeStruct((GROUPS, PA...  17 us
    pallas_call x1, Pallas kernels, normalise(): pl.pallas_call(norm_kernel, out_shape=jax.ShapeDtypeStruct((8, 128), jnp....  8.53 us
    pallas_call x1, Pallas kernels, score_slots(): pl.pallas_call(score_kernel, out_shape=(jax.ShapeDtypeStruct((SLOTS, 8, 2...  8.15 us
    pallas_call x1, Pallas kernels, sum_slots(): pl.pallas_call(sum_kernel, out_shape=jax.ShapeDtypeStruct((NCH, 4, 8, RC,...  4.34 us
    reshape x1, local copies, waits for them, and re-layouts, unpack_average(): return rows.reshape(CLS_LOC, 36864)  2.24 us

profile of v5, /device:TPU:8, one launch (start us, length us, event | category | flops | bytes accessed | tf_op | source)
XLA Modules:
  0.0 94.3 jit_solution(17484766667107797679)
XLA Ops:
  0.0 1.0 %copy.9 = bf16[1,4,288,128]{3,2,1,0:T(8,128)(2,1)S(1)} copy(bf16[1,4,288,128]{3,1,2,0:T(4,128)(2,1)} %bitcast.12) | data formatting | bytes 589824
  1.0 17.0 %gather_particles.1 = (bf16[8,4,288,128]{3,2,1,0:T(8,128)(2,1)S(1)}, s32[8,4,8]{2,1,0:T(4,128)S(1)}, s32[8,2,4]{2,1,0:T(2,128)S(1)}, bf16[25,48,1024]{2,1,0:T(8,128)(2,1)S(1)}, f32[2,8,2,4,40,128]{5,4,3,2,1,0:T(8,128)S(1)}) custom-call(bf16[4,288,128]{2,1,0:T(8,128)(2,1)S(1)} %bitcast.10, s32[4,8]{1,0:T(4,128)} %cand_ref.1, s32[2,4]{1,0:T(2,128)} %bitcast.13, ...), custom_call_target="tpu_custom_call" | custom-call | tf_op jit(solution)/shard_map/gather_particles/pallas_call | solution.py:120
  18.1 8.2 %score_slots.1 = (f32[16,8,256]{2,1,0:T(8,128)S(1)}, bf16[16,256,1024]{2,1,0:T(8,128)(2,1)S(1)}, f32[8,128]{1,0:T(8,128)S(1)}, s32[136]{0:T(256)S(1)}) custom-call(s32[8,4,8]{2,1,0:T(4,128)S(1)} %get-tuple-element.14.cands, s32[8,2,4]{2,1,0:T(2,128)S(1)} %get-tuple-element.15.priors, f32[2,8,2,4,40,128]{5,4,3,2,1,0:T(8,128)S(1)} %get-tuple-element.16.powers, ...), custom_call_target="tpu_custom_call" | custom-call | tf_op jit(solution)/shard_map/score_slots/pallas_call | solution.py:230
  26.2 8.5 %normalise.1.total = f32[8,128]{1,0:T(8,128)S(1)} custom-call(f32[8,128]{1,0:T(8,128)S(1)} %get-tuple-element.20.stats), custom_call_target="tpu_custom_call" | custom-call | tf_op jit(solution)/shard_map/normalise/pallas_call | solution.py:272
  34.7 4.3 %sum_slots.1.p_ref = bf16[5,4,8,48,128]{4,3,2,1,0:T(8,128)(2,1)S(1)} custom-call(s32[136]{0:T(256)S(1)} %get-tuple-element.19.table, f32[8,128]{1,0:T(8,128)S(1)} %normalise.1.total, f32[16,8,256]{2,1,0:T(8,128)S(1)} %get-tuple-element.21.scores, bf16[16,256,1024]{2,1,0:T(8,128)(2,1)S(1)} %get-tuple-element.22.moved), custom_call_target="tpu_custom_call" | custom-call | tf_op jit(solution)/shard_map/sum_slots/pallas_call | solution.py:352
  39.1 52.3 %reduce_average.1 = bf16[5,4,8,48,128]{4,3,2,1,0:T(8,128)(2,1)S(1)} custom-call(bf16[5,4,8,48,128]{4,3,2,1,0:T(8,128)(2,1)S(1)} %sum_slots.1.p_ref), custom_call_target="tpu_custom_call" | custom-call | tf_op jit(solution)/shard_map/reduce_average/pallas_call | solution.py:482
  91.4 0.5 copy.6
  92.0 0.1 slice.4
  92.1 2.2 %reshape.11 = bf16[25,36864]{1,0:T(8,128)(2,1)} reshape(bf16[4,225,8,128]{3,2,1,0:T(8,128)(2,1)S(1)} %slice.4) | data formatting | bytes 3686400 | tf_op jit(solution)/shard_map/reshape | solution.py:502
